TPU v7x, 128 devices: a whole 4x4x4 slice. The times are simulated.
128 devices in a mesh: row: 16 (over y, z), col: 8 (over x, core).
Axes of the slice: x: 4, y: 4, z: 4, core: 2. Of those that a mesh axis runs over, the one named last changes fastest.
Arguments:
- momentum: float32 [8192, 16384], P('row', 'col'), may hold values from -6 to 6
- grads: bfloat16 [2, 8192, 16384], P(None, 'row', 'col'), may hold values from -400 to 400
- basis: float32 [16384, 256], P('col'), may hold values from -0.046875 to 0.046875
Outputs:
- change: bfloat16 [8192, 16384], P('row', 'col')
- state: float32 [8192, 16384], P('row', 'col')
All inputs are finite; a program needn't handle non-finite values.
Results may differ from a plain program's by a relative error of at most 0.0035.
Values sent between devices are 32-bit elements; how exact they have to be, the bound alone decides.
No kernel may reach another device: no remote copies, remote signals or barrier semaphores. Data moves between devices by JAX's collectives and lax.ppermute only.
A program may use at most 128 MiB of HBM per device.

v0:
```python
import jax
import jax.numpy as jnp
from jax import lax
from jax.sharding import PartitionSpec as P

ROWS = 8192
COLS = 16384
RANK = 256
STEPS = 2


keep_rate = 0.95
norm_eps = 1e-06


def over_pieces(shard, axis):
    parts = lax.all_gather(shard, axis)
    return parts.sum(axis=0)


def filled_up(lines, count):
    spare = -len(lines) % count
    return jnp.pad(lines, [(0, spare)] + [(0, 0)] * (lines.ndim - 1))


def laid_out(parts, dim):
    parts = jnp.moveaxis(parts, 0, dim)
    dims = parts.shape
    return parts.reshape(*dims[:dim], dims[dim] * dims[dim + 1], *dims[dim + 2 :])


def copy_for_each(shard, axis):
    count = lax.axis_size(axis)
    return lax.all_to_all(
        jnp.broadcast_to(shard[None], (count, *shard.shape)), axis, 0, 0, tiled=True
    )


def collect(shard, axis, dim):
    return laid_out(copy_for_each(shard, axis), dim)


def split_up(shard, dim, count):
    dims = shard.shape
    parts = shard.reshape(*dims[:dim], count, dims[dim] // count, *dims[dim + 1 :])
    return jnp.moveaxis(parts, dim, 0)


def sent_and_summed(shard, axis, dim):
    count = lax.axis_size(axis)
    parts = lax.all_to_all(split_up(shard, dim, count), axis, 0, 0, tiled=True)
    return jnp.sum(parts, axis=0)


def total_of(shard, axes):
    lines = shard.reshape(-1, shard.shape[-1])
    padded = filled_up(lines, lax.axis_size(axes))
    whole = collect(sent_and_summed(padded, axes, 0), axes, 0)
    return lax.slice_in_dim(whole, 0, len(lines)).reshape(shard.shape)


def of_everyone(shard, axis):
    return copy_for_each(shard, axis).sum(axis=0)


def column_squares(matrix):
    return jnp.sum(matrix * matrix, axis=0)


def shards(momentum, grads, basis):
    high = lax.Precision.HIGHEST
    factor = (ROWS * COLS / RANK) ** 0.5
    state = momentum
    right = basis
    change = jnp.zeros(momentum.shape, jnp.float32)
    for step in range(STEPS):
        buffer = state + grads[step].astype(jnp.float32)
        partial_value = jnp.dot(buffer, right, precision=high, preferred_element_type=jnp.float32)
        projected = over_pieces(partial_value, "col")
        gram = total_of(
            jnp.dot(projected.T, projected, precision=high, preferred_element_type=jnp.float32),
            "row",
        )
        lower = jnp.linalg.cholesky(gram)
        ortho = jax.scipy.linalg.solve_triangular(lower, projected.T, lower=True).T
        local_right = lax.dot_general(
            buffer,
            ortho,
            (((0,), (0,)), ((), ())),
            precision=high,
            preferred_element_type=jnp.float32,
        )
        raw = total_of(local_right, "row")
        squares = of_everyone(column_squares(raw), "col")
        right = raw * lax.rsqrt(squares + norm_eps)
        state = buffer - (1.0 - keep_rate) * jnp.dot(
            ortho, raw.T, precision=high, preferred_element_type=jnp.float32
        )
        change = change + factor * jnp.dot(
            ortho, right.T, precision=high, preferred_element_type=jnp.float32
        )
    return (change.astype(jnp.bfloat16), state)


def solution(mesh):
    return jax.shard_map(
        shards,
        mesh=mesh,
        in_specs=(P("row", "col"), P(None, "row", "col"), P("col", None)),
        out_specs=(P("row", "col"), P("row", "col")),
        check_vma=False,
    )
```

profile of v0, /device:TPU:1, one launch (start us, length us, event | category | flops | bytes accessed | tf_op | source)
XLA Modules:
  0.0 471.7 jit_solution(9924420847645025015)
XLA Ops:
  7.2 1.5 copy-done
  8.8 6.4 %fusion.6 = f32[512,256]{1,0:T(8,128)} fusion(f32[2048,256]{1,0:T(8,128)S(1)} %copy-done, f32[512,2048]{1,0:T(8,128)} %param.6, bf16[2,512,2048]{2,1,0:T(8,128)(2,1)} %param.7), kind=kOutput, calls=%fused_computation.20 | convolution fusion | flops 3223322624 | bytes 8912896 | tf_op jit(solution)/shard_map/dot_general | solution.py:78
  15.2 35.9 %all-gather.5.cloned.1.call-done = f32[4096,256]{1,0:T(8,128)} async-done(((f32[512,256]{1,0:T(8,128)}), f32[4096,256]{1,0:T(8,128)}) %all-gather.5.cloned.1.call-update) | async-done | bytes 4194320 | tf_op jit(solution)/shard_map/all_gather | solution.py:17
  51.1 2.5 reduce_sum.90
  54.4 14.2 %all_to_all.52 = f32[16,16,256]{2,1,0:T(8,128)S(1)} all-to-all(f32[16,16,256]{2,1,0:T(8,128)S(1)} %fusion.12), channel_id=1, replica_groups=mesh['row'=16,'col'=8] {'row'}, dimensions={0} | all-to-all | bytes 524288 | tf_op jit(solution)/shard_map/all_to_all | solution.py:51
  68.6 0.7 broadcast_in_dim.13
  69.3 3.9 all-to-all-start.1
  73.2 7.3 %all-to-all-done.1 = f32[16,16,256]{2,1,0:T(8,128)S(1)} async-done(((f32[16,16,256]{2,1,0:T(8,128)}), f32[16,16,256]{2,1,0:T(8,128)S(1)}, u32[]{:S(2)}, u32[]{:S(2)}) %all-to-all-start.1) | async-done | bytes 262176 | tf_op jit(solution)/shard_map/all_to_all | solution.py:34
  80.7 11.7 %cholesky.130 = f32[128,128]{1,0:T(8,128)S(1)} custom-call(f32[128,128]{1,0:T(8,128)S(1)} %cholesky.194), custom_call_target="Cholesky" | custom-call | tf_op jit(solution)/shard_map/jit(cholesky)/cholesky | solution.py:84
  92.5 9.8 %custom-call.13 = f32[1,128,128]{1,2,0:T(8,128)S(1)} custom-call(f32[1,128,128]{2,1,0:T(8,128)S(1)} %get-tuple-element.47), custom_call_target="InvertDiagBlocksLowerTriangular" | custom-call | tf_op jit(solution)/shard_map/jit(cholesky)/cholesky | solution.py:84
  102.8 11.7 %cholesky.147 = f32[128,128]{1,0:T(8,128)S(1)} custom-call(f32[128,128]{1,0:T(8,128)S(1)} %convolution_subtract_fusion.3), custom_call_target="Cholesky" | custom-call | tf_op jit(solution)/shard_map/jit(cholesky)/cholesky | solution.py:84
  114.5 0.7 compare_reduce_fusion.2
  116.7 4.1 while.4
  117.3 1.4 bitcast_dynamic-update-slice_fusion.4
  119.4 1.4 bitcast_dynamic-update-slice_fusion.4
  120.8 19.9 %custom-call.14 = f32[2,128,128]{1,2,0:T(8,128)S(1)} custom-call(f32[2,128,128]{2,1,0:T(8,128)S(1)} %get-tuple-element.18), custom_call_target="InvertDiagBlocksLowerTriangular" | custom-call | tf_op jit(solution)/shard_map/jit(_solve_triangular)/triangular_solve | solution.py:85
  142.0 8.9 %fusion.5 = f32[2048,256]{1,0:T(8,128)S(1)} fusion(f32[512,2048]{1,0:T(8,128)} %param.6, bf16[2,512,2048]{2,1,0:T(8,128)(2,1)} %param.7, f32[128,512]{1,0:T(8,128)S(1)} %fusion.26, f32[128,512]{1,0:T(8,128)S(1)} %fusion.17), kind=kOutput, calls=%fused_computation.19 | convolution fusion | flops 3223453696 | bytes 8912896 | tf_op jit(solution)/shard_map/dot_general | solution.py:86
  150.9 28.1 %all_to_all.53 = f32[16,128,256]{2,1,0:T(8,128)} all-to-all(f32[16,128,256]{2,1,0:T(8,128)S(1)} %bitcast.104), channel_id=1, replica_groups=mesh['row'=16,'col'=8] {'row'}, dimensions={0} | all-to-all | bytes 4194304 | tf_op jit(solution)/shard_map/all_to_all | solution.py:51
  179.0 1.7 reduce_sum.92
  181.0 28.0 %all_to_all.54 = f32[16,128,256]{2,1,0:T(8,128)S(1)} all-to-all(f32[16,128,256]{2,1,0:T(8,128)S(1)} %broadcast_in_dim.14), channel_id=1, replica_groups=mesh['row'=16,'col'=8] {'row'}, dimensions={0} | all-to-all | bytes 4194304 | tf_op jit(solution)/shard_map/all_to_all | solution.py:34
  208.9 1.3 copy-done.1
  211.1 8.5 %all-to-all-start.4 = ((f32[8,1,256]{2,1,0:T(1,128)}), f32[8,1,256]{2,1,0:T(1,128)S(1)}, u32[]{:S(2)}, u32[]{:S(2)}) async-start(f32[8,1,256]{2,1,0:T(1,128)} %broadcast_in_dim.15), calls=%async_computation.4 | async-start | bytes 16384 | tf_op jit(solution)/shard_map/all_to_all | solution.py:34
  219.7 12.4 %convert_add_fusion = f32[512,2048]{1,0:T(8,128)} fusion(f32[2048,256]{1,0:T(8,128)} %bitcast.101, bf16[2,512,2048]{2,1,0:T(8,128)(2,1)} %param.7, f32[512,2048]{1,0:T(8,128)} %param.6, f32[128,512]{1,0:T(8,128)S(1)} %fusion.26, f32[128,512]{1,0:T(8,128)S(1)} %fusion.17), kind=kOutput, calls=%fused_computation.4 | convolution fusion | flops 3227648000 | bytes 15204352 | tf_op jit(solution)/shard_map/dot_general | solution.py:96
  232.1 7.1 %fusion.1 = f32[512,256]{1,0:T(8,128)} fusion(f32[512,2048]{1,0:T(8,128)} %convert_add_fusion, f32[2048,256]{1,0:T(8,128)} %bitcast.102, f32[256]{0:T(256)S(1)} %add_rsqrt_fusion.1), kind=kOutput, calls=%fused_computation.11 | convolution fusion | flops 3221749760 | bytes 6816768 | tf_op jit(solution)/shard_map/dot_general | solution.py:78
  239.3 30.3 %all-gather.7.cloned.1.call-done = f32[4096,256]{1,0:T(8,128)} async-done(((f32[512,256]{1,0:T(8,128)}), f32[4096,256]{1,0:T(8,128)}) %all-gather.7.cloned.1.call-update) | async-done | bytes 4194320 | tf_op jit(solution)/shard_map/all_gather | solution.py:17
  269.6 2.5 reduce_sum.95
  272.9 14.2 %all_to_all.55 = f32[16,16,256]{2,1,0:T(8,128)S(1)} all-to-all(f32[16,16,256]{2,1,0:T(8,128)S(1)} %fusion.10), channel_id=1, replica_groups=mesh['row'=16,'col'=8] {'row'}, dimensions={0} | all-to-all | bytes 524288 | tf_op jit(solution)/shard_map/all_to_all | solution.py:51
  287.2 11.0 %all_to_all.56 = f32[16,16,256]{2,1,0:T(8,128)S(1)} all-to-all(f32[16,16,256]{2,1,0:T(8,128)S(1)} %broadcast_in_dim.16), channel_id=1, replica_groups=mesh['row'=16,'col'=8] {'row'}, dimensions={0} | all-to-all | bytes 524288 | tf_op jit(solution)/shard_map/all_to_all | solution.py:34
  299.1 11.7 %cholesky.164 = f32[128,128]{1,0:T(8,128)S(1)} custom-call(f32[128,128]{1,0:T(8,128)S(1)} %cholesky.197), custom_call_target="Cholesky" | custom-call | tf_op jit(solution)/shard_map/jit(cholesky)/cholesky | solution.py:84
  310.8 9.8 %custom-call.15 = f32[1,128,128]{1,2,0:T(8,128)S(1)} custom-call(f32[1,128,128]{2,1,0:T(8,128)S(1)} %get-tuple-element.43), custom_call_target="InvertDiagBlocksLowerTriangular" | custom-call | tf_op jit(solution)/shard_map/jit(cholesky)/cholesky | solution.py:84
  320.6 1.0 constant_dynamic-update-slice_fusion.1
  321.7 1.1 convolution_subtract_fusion.2
  322.8 11.7 %cholesky.181 = f32[128,128]{1,0:T(8,128)S(1)} custom-call(f32[128,128]{1,0:T(8,128)S(1)} %convolution_subtract_fusion.2), custom_call_target="Cholesky" | custom-call | tf_op jit(solution)/shard_map/jit(cholesky)/cholesky | solution.py:84
  337.3 4.2 while.5
  338.0 1.4 bitcast_dynamic-update-slice_fusion.5
  340.1 1.4 bitcast_dynamic-update-slice_fusion.5
  341.5 19.9 %custom-call.16 = f32[2,128,128]{1,2,0:T(8,128)S(1)} custom-call(f32[2,128,128]{2,1,0:T(8,128)S(1)} %get-tuple-element.19), custom_call_target="InvertDiagBlocksLowerTriangular" | custom-call | tf_op jit(solution)/shard_map/jit(_solve_triangular)/triangular_solve | solution.py:85
  362.6 8.5 %fusion.14 = f32[2048,256]{1,0:T(8,128)S(1)} fusion(f32[512,2048]{1,0:T(8,128)} %convert_add_fusion, f32[128,512]{1,0:T(8,128)S(1)} %fusion.22, f32[128,512]{1,0:T(8,128)S(1)} %fusion.15), kind=kOutput, calls=%fused_computation.30 | convolution fusion | flops 3221356544 | bytes 6815744 | tf_op jit(solution)/shard_map/dot_general | solution.py:86
  371.1 28.2 %all_to_all.57 = f32[16,128,256]{2,1,0:T(8,128)} all-to-all(f32[16,128,256]{2,1,0:T(8,128)S(1)} %bitcast.105), channel_id=1, replica_groups=mesh['row'=16,'col'=8] {'row'}, dimensions={0} | all-to-all | bytes 4194304 | tf_op jit(solution)/shard_map/all_to_all | solution.py:51
  399.3 1.8 reduce_sum.97
  401.0 1.5 broadcast_in_dim.17
  402.6 4.4 all-to-all-start.8
  407.0 10.0 %fusion.3 = f32[512,2048]{1,0:T(8,128)} fusion(f32[2048,256]{1,0:T(8,128)} %bitcast.103, f32[256]{0:T(256)S(1)} %add_rsqrt_fusion.1, f32[128,512]{1,0:T(8,128)S(1)} %copy-done.3, f32[128,512]{1,0:T(8,128)S(1)} %fusion.17), kind=kOutput, calls=%fused_computation.13 | convolution fusion | flops 3221880832 | bytes 6816768 | tf_op jit(solution)/shard_map/dot_general | solution.py:99
  417.0 13.7 %all-to-all-done.8 = f32[16,128,256]{2,1,0:T(8,128)} async-done(((f32[16,128,256]{2,1,0:T(8,128)}), f32[16,128,256]{2,1,0:T(8,128)}, u32[]{:S(2)}, u32[]{:S(2)}) %all-to-all-start.8) | async-done | bytes 2097184 | tf_op jit(solution)/shard_map/all_to_all | solution.py:34
  430.7 1.9 multiply_reduce_fusion
  433.2 10.3 %all-to-all-start.9 = ((f32[8,1,256]{2,1,0:T(1,128)}), f32[8,1,256]{2,1,0:T(1,128)S(1)}, u32[]{:S(2)}, u32[]{:S(2)}) async-start(f32[8,1,256]{2,1,0:T(1,128)} %broadcast_in_dim.18), calls=%async_computation.9 | async-start | bytes 16384 | tf_op jit(solution)/shard_map/all_to_all | solution.py:34
  443.5 10.7 %multiply_subtract_fusion = f32[512,2048]{1,0:T(8,128)} fusion(f32[512,2048]{1,0:T(8,128)} %convert_add_fusion, f32[2048,256]{1,0:T(8,128)} %bitcast.25, f32[128,512]{1,0:T(8,128)S(1)} %fusion.22, f32[128,512]{1,0:T(8,128)S(1)} %fusion.15), kind=kOutput, calls=%fused_computation.7 | convolution fusion | flops 3223453696 | bytes 11010048 | tf_op jit(solution)/shard_map/dot_general | solution.py:96
  454.2 10.4 %multiply_convert_fusion = bf16[512,2048]{1,0:T(8,128)(2,1)} fusion(f32[512,2048]{1,0:T(8,128)} %fusion.3, f32[2048,256]{1,0:T(8,128)} %bitcast.25, f32[256]{0:T(256)S(1)} %add_rsqrt_fusion, f32[128,512]{1,0:T(8,128)S(1)} %fusion.22, f32[128,512]{1,0:T(8,128)S(1)} %fusion.15), kind=kOutput, calls=%fused_computation.6 | convolution fusion | flops 3225026560 | bytes 8913920 | tf_op jit(solution)/shard_map/dot_general | solution.py:99
  (65 shorter events, 11.7 us)
Async XLA Ops:
  7.2 1.6 copy-start
  7.2 43.9 %all-gather.5.cloned.1.call-start = ((), (), s32[]{:S(2)}) async-start(), calls=%async_computation.10 | async-start | bytes 4718592 | tf_op jit(solution)/shard_map/all_gather | solution.py:17
  69.3 11.2 %all-to-all-start.1 = ((f32[16,16,256]{2,1,0:T(8,128)}), f32[16,16,256]{2,1,0:T(8,128)S(1)}, u32[]{:S(2)}, u32[]{:S(2)}) async-start(f32[16,16,256]{2,1,0:T(8,128)} %broadcast_in_dim.13), calls=%async_computation.1 | async-start | bytes 524288 | tf_op jit(solution)/shard_map/all_to_all | solution.py:34
  142.0 77.7 %copy-start.2 = (f32[128,512]{1,0:T(8,128)}, f32[128,512]{1,0:T(8,128)S(1)}, u32[]{:S(2)}) copy-start(f32[128,512]{1,0:T(8,128)S(1)} %fusion.26) | copy-start | bytes 786436
  208.9 1.3 copy-start.1
  211.1 20.9 %all-to-all-start.4 = ((f32[8,1,256]{2,1,0:T(1,128)}), f32[8,1,256]{2,1,0:T(1,128)S(1)}, u32[]{:S(2)}, u32[]{:S(2)}) async-start(f32[8,1,256]{2,1,0:T(1,128)} %broadcast_in_dim.15), calls=%async_computation.4 | async-start | bytes 16384 | tf_op jit(solution)/shard_map/all_to_all | solution.py:34
  219.7 49.9 %all-gather.7.cloned.1.call-start = ((), (), s32[]{:S(2)}) async-start(), calls=%async_computation.11 | async-start | bytes 4718592 | tf_op jit(solution)/shard_map/all_gather | solution.py:17
  298.4 0.7 copy-start.4
  399.3 7.8 %copy-start.3 = (f32[128,512]{1,0:T(8,128)S(1)}, f32[128,512]{1,0:T(8,128)}, u32[]{:S(2)}) copy-start(f32[128,512]{1,0:T(8,128)} %copy-done.2) | copy-start | bytes 786436
  402.6 28.1 %all-to-all-start.8 = ((f32[16,128,256]{2,1,0:T(8,128)}), f32[16,128,256]{2,1,0:T(8,128)}, u32[]{:S(2)}, u32[]{:S(2)}) async-start(f32[16,128,256]{2,1,0:T(8,128)} %broadcast_in_dim.17), calls=%async_computation.8 | async-start | bytes 4194304 | tf_op jit(solution)/shard_map/all_to_all | solution.py:34
  433.2 21.0 %all-to-all-start.9 = ((f32[8,1,256]{2,1,0:T(1,128)}), f32[8,1,256]{2,1,0:T(1,128)S(1)}, u32[]{:S(2)}, u32[]{:S(2)}) async-start(f32[8,1,256]{2,1,0:T(1,128)} %broadcast_in_dim.18), calls=%async_computation.9 | async-start | bytes 16384 | tf_op jit(solution)/shard_map/all_to_all | solution.py:34
Sparse Core Ops, SparseCore 0:
  15.3 35.6 all-gather.4
  239.4 30.1 all-gather.6
where the time goes:
time: 476 us; the launch traced here: 472 us
  blocking collectives  124 us (26%)
  other arithmetic  119 us (25%)
  waiting for transfers between devices  87.2 us (18%)
  matrix products  80.6 us (17%)
  starting transfers between devices  27.2 us (6%)
  between operations  17.3 us (4%)
  local copies, waits for them, and re-layouts  16.2 us (3%)
    all_to_all x4, blocking collectives, sent_and_summed(): parts = lax.all_to_all(split_up(shard, dim, count), axis, 0, 0, tiled=True)  84.7 us
    another operation x13, other arithmetic, shards(): lower = jnp.linalg.cholesky(gram)  68.7 us
    all_gather x2, waiting for transfers between devices, over_pieces(): parts = lax.all_gather(shard, axis)  66.2 us
    another operation x5, other arithmetic, shards(): ortho = jax.scipy.linalg.solve_triangular(lower, projected.T, lower=True).T  39.8 us
    all_to_all x2, blocking collectives, copy_for_each(): lax.all_to_all(jnp.broadcast_to(shard[None], (count, *shard.shape)), axis...  39 us
    all_to_all x4, starting transfers between devices, copy_for_each(): lax.all_to_all(jnp.broadcast_to(shard[None], (count, *shard.shape)), axis...  27.2 us
    dot_general x2, matrix products, shards(): jnp.dot(ortho, raw.T, precision=high, preferred_element_type=jnp.float32)  23.1 us
    all_to_all x4, waiting for transfers between devices, copy_for_each(): lax.all_to_all(jnp.broadcast_to(shard[None], (count, *shard.shape)), axis...  21 us
  transfers between devices with their start and end apart: 6, of which 4 were waited for; matrix products, arithmetic and copies ran while one was open for 7% of the time, Pallas kernels for 0%

commit v1 on v0

v1 whole, which is shorter than its diff:
```python
import functools

import jax
import jax.numpy as jnp
from jax import lax
from jax.experimental import pallas as pl
from jax.experimental.pallas import tpu as pltpu
from jax.sharding import PartitionSpec as P

KEEP_RATE = 0.95
NORM_EPS = 1e-06
STEPS = 2
LANES = 128
F32 = jnp.float32
BF16 = jnp.bfloat16
VMEM_LIMIT = 48 * 1024 * 1024
NN = (((1,), (0,)), ((), ()))
NT = (((1,), (1,)), ((), ()))


def split(x):
    high = x.astype(BF16)
    return high, (x - high.astype(F32)).astype(BF16)


def mm(a, b, dims):
    return lax.dot_general(a, b, dims, preferred_element_type=F32)


def dot3(a, b, dims):
    return mm(a[0], b[0], dims) + (mm(a[0], b[1], dims) + mm(a[1], b[0], dims))


def exact(a, b, dims):
    return lax.dot_general(
        a, b, dims, precision=lax.Precision.HIGHEST, preferred_element_type=F32
    )


def call(kernel, grid, in_specs, out_specs, out_shape, scratch, cost):
    return pl.pallas_call(
        kernel,
        grid=grid,
        in_specs=in_specs,
        out_specs=out_specs,
        out_shape=out_shape,
        scratch_shapes=scratch,
        compiler_params=pltpu.CompilerParams(vmem_limit_bytes=VMEM_LIMIT),
        cost_estimate=pl.CostEstimate(
            flops=cost, transcendentals=0, bytes_accessed=8 * 1024 * 1024
        ),
    )


def whole(shape):
    return pl.BlockSpec(shape, lambda i: (0,) * len(shape))


def first_kernel(m_ref, g_ref, v_ref, p_ref, vh, vl):
    @pl.when(pl.program_id(0) == 0)
    def _():
        vh[...], vl[...] = split(v_ref[...])

    b = split(m_ref[...] + g_ref[0].astype(F32))
    p_ref[...] = dot3(b, (vh[...], vl[...]), NN)


def first_projection(momentum, grads, basis):
    rows, cols = momentum.shape
    rank = basis.shape[1]
    bm = rows // 4
    return call(
        first_kernel,
        (4,),
        [
            pl.BlockSpec((bm, cols), lambda i: (i, 0)),
            pl.BlockSpec((1, bm, cols), lambda i: (0, i, 0)),
            whole(basis.shape),
        ],
        pl.BlockSpec((bm, rank), lambda i: (i, 0)),
        jax.ShapeDtypeStruct((rows, rank), F32),
        [pltpu.VMEM(basis.shape, BF16)] * 2,
        6 * rows * cols * rank,
    )(momentum, grads, basis)


def store_products(p, b, x_ref, pt, gram, blocks):
    rank = p.shape[1]
    share = rank // 16

    @pl.when(pl.program_id(0) == 0)
    def _():
        turned = p.T
        pt[0], pt[1] = split(turned)
        gram[...] = exact(turned, p, NN)

    r = dot3((pt[0], pt[1]), split(b), NN)
    for k in range(blocks):
        x_ref[k, :rank] = r[:, k * LANES : (k + 1) * LANES]
        first = pl.multiple_of((pl.program_id(0) * blocks + k) * share, share)
        for part in range(rank // LANES):
            x_ref[k, rank + part * share : rank + (part + 1) * share] = gram[
                pl.ds(first, share), part * LANES : (part + 1) * LANES
            ]


def raw_first_kernel(blocks, p_ref, m_ref, g_ref, x_ref, pt, gram):
    store_products(
        p_ref[...], m_ref[...] + g_ref[0].astype(F32), x_ref, pt, gram, blocks
    )


def raw_second_kernel(blocks, p_ref, rs_ref, b_ref, x_ref, pt, gram):
    store_products(p_ref[...] * rs_ref[:1], b_ref[...], x_ref, pt, gram, blocks)


def raw_products(kernel, p, small, bigs, big_specs, cols):
    rows, rank = p.shape
    blocks = 4
    steps = cols // LANES // blocks
    height = rank + rank * (rank // 16) // LANES
    return call(
        functools.partial(kernel, blocks),
        (steps,),
        [whole(p.shape)] + [whole(s.shape) for s in small] + big_specs(rows, blocks * LANES),
        pl.BlockSpec((blocks, height, LANES), lambda i: (i, 0, 0)),
        jax.ShapeDtypeStruct((cols // LANES, height, LANES), F32),
        [pltpu.VMEM((2, rank, rows), BF16), pltpu.VMEM((rank, rank), F32)],
        6 * rows * cols * rank,
    )(p, *small, *bigs)


def eliminated(m):
    n = m.shape[0]
    lane = lax.broadcasted_iota(jnp.int32, (8, n), 1)
    sub = lax.broadcasted_iota(jnp.int32, (8, n), 0)
    tiles = [m[8 * t : 8 * t + 8] for t in range(n // 8)]
    for j in range(n):
        t, r = divmod(j, 8)
        row = tiles[t][r : r + 1]
        inv = 1.0 / row[:, j : j + 1]
        here = lane == j
        scaled = jnp.where(here[:1], inv, row * inv)
        for s in range(t, n // 8):
            column = jnp.broadcast_to(tiles[s][:, j : j + 1], (8, n))
            new = jnp.where(here, 0.0, tiles[s]) - column * scaled
            if s == t:
                new = jnp.where(sub > r, new, tiles[s])
            tiles[s] = new
    m = jnp.concatenate(tiles, axis=0)
    i = lax.broadcasted_iota(jnp.int32, (n, n), 0)
    j = lax.broadcasted_iota(jnp.int32, (n, n), 1)
    pivots = jnp.sum(jnp.where(i == j, m, 0.0), axis=1, keepdims=True)
    unit = jnp.where(i > j, m, jnp.where(i == j, 1.0, 0.0))
    return unit * lax.rsqrt(pivots)


def cholesky_kernel(g_ref, w_ref, a, low):
    count, height, _ = g_ref.shape
    share = height // 2
    half = LANES
    for k in range(count):
        for part in range(2):
            a[k * share : (k + 1) * share, part * half : (part + 1) * half] = g_ref[
                k, part * share : (part + 1) * share
            ]

    def body(b, carry):
        first = pl.multiple_of(b * half, half)
        w = eliminated(a[pl.ds(first, half), pl.ds(first, half)])
        w_ref[pl.ds(first, half), pl.ds(first, half)] = w

        @pl.when(b == 0)
        def _():
            low[...] = exact(a[half:, :half], w, NT)
            a[half:, half:] -= exact(low[...], low[...], NT)

        return carry

    lax.fori_loop(0, 2, body, 0)
    w_ref[:half, half:] = jnp.zeros((half, half), F32)
    w_ref[half:, :half] = -exact(
        w_ref[half:, half:], exact(low[...], w_ref[:half, :half], NN), NN
    )


def inverse_factor(gram):
    rank = 2 * LANES
    return call(
        cholesky_kernel,
        (1,),
        [whole(gram.shape)],
        whole((rank, rank)),
        jax.ShapeDtypeStruct((rank, rank), F32),
        [pltpu.VMEM((rank, rank), F32), pltpu.VMEM((LANES, LANES), F32)],
        10**10,
    )(gram)


def assemble_raw(w_ref, x_ref, raw_ref):
    count = x_ref.shape[0]
    w = split(w_ref[...])
    for k in range(0, count, 4):
        block = jnp.concatenate([x_ref[k + q] for q in range(4)], axis=1)
        raw_ref[:, k * LANES : (k + 4) * LANES] = dot3(w, split(block), NN)


def squares_of(raw):
    return jnp.sum(raw * raw, axis=1, keepdims=True)


def middle_kernel(p_ref, w_ref, x_ref, m_ref, g_ref, q_ref, raw_ref, o_ref, rt, s_ref):
    bm = m_ref.shape[0]
    step = pl.program_id(0)

    @pl.when(step == 0)
    def _():
        assemble_raw(w_ref, x_ref, raw_ref)
        raw = raw_ref[...]
        rt[0], rt[1] = split(raw)
        s = dot3((rt[0], rt[1]), (rt[0], rt[1]), NT)
        s_ref[...] = s
        o_ref[...] = exact(p_ref[...], w_ref[...], NT)
        n = s.shape[0]
        i = lax.broadcasted_iota(jnp.int32, (n, n), 0)
        j = lax.broadcasted_iota(jnp.int32, (n, n), 1)
        squares = jnp.sum(jnp.where(i == j, s, 0.0), axis=0, keepdims=True)
        for half in range(2):
            q_ref[half, q_ref.shape[1] - 8 :] = jnp.broadcast_to(squares, (8, n))

    b = m_ref[...] + g_ref[0].astype(F32) + g_ref[1].astype(F32)
    q = dot3(split(b), (rt[0], rt[1]), NT)
    first = pl.multiple_of(step * bm, bm)
    o = o_ref[pl.ds(first, bm), :]
    q = q - (1.0 - KEEP_RATE) * exact(o, s_ref[...], NN)
    per_half = (q_ref.shape[1] - 8) // bm
    q_ref[step // per_half, pl.ds(pl.multiple_of((step % per_half) * bm, bm), bm), :] = q


def middle(p, w, x, momentum, grads):
    rows, cols = momentum.shape
    rank = p.shape[1]
    bm = rows // 4
    return call(
        middle_kernel,
        (4,),
        [
            whole(p.shape),
            whole(w.shape),
            whole(x.shape),
            pl.BlockSpec((bm, cols), lambda i: (i, 0)),
            pl.BlockSpec((2, bm, cols), lambda i: (0, i, 0)),
        ],
        [whole((2, rows // 2 + 8, rank)), whole((rank, cols)), whole((rows, rank))],
        [
            jax.ShapeDtypeStruct((2, rows // 2 + 8, rank), F32),
            jax.ShapeDtypeStruct((rank, cols), F32),
            jax.ShapeDtypeStruct((rows, rank), F32),
        ],
        [pltpu.VMEM((2, rank, cols), BF16), pltpu.VMEM((rank, rank), F32)],
        10 * rows * cols * rank,
    )(p, w, x, momentum, grads)


def update_kernel(o_ref, raw_ref, m_ref, g_ref, b_ref):
    b = m_ref[...] + g_ref[0].astype(F32) + g_ref[1].astype(F32)
    o = split((1.0 - KEEP_RATE) * o_ref[...])
    b_ref[...] = b - dot3(o, split(raw_ref[...]), NN)


def second_buffer(o, raw, momentum, grads):
    rows, cols = momentum.shape
    rank = o.shape[1]
    bn = cols // 4
    return call(
        update_kernel,
        (4,),
        [
            whole(o.shape),
            pl.BlockSpec((rank, bn), lambda i: (0, i)),
            pl.BlockSpec((rows, bn), lambda i: (0, i)),
            pl.BlockSpec((2, rows, bn), lambda i: (0, 0, i)),
        ],
        pl.BlockSpec((rows, bn), lambda i: (0, i)),
        jax.ShapeDtypeStruct((rows, cols), F32),
        [],
        6 * rows * cols * rank,
    )(o, raw, momentum, grads)


def change_kernel(factor, o_ref, rs_ref, raw_ref, c_ref):
    o = split(o_ref[...] * (factor * rs_ref[:1]))
    c_ref[...] = dot3(o, split(raw_ref[...]), NN)


def first_change(factor, o, rs, raw):
    rows, rank = o.shape
    cols = raw.shape[1]
    bn = cols // 4
    return call(
        functools.partial(change_kernel, factor),
        (4,),
        [whole(o.shape), whole(rs.shape), pl.BlockSpec((rank, bn), lambda i: (0, i))],
        pl.BlockSpec((rows, bn), lambda i: (0, i)),
        jax.ShapeDtypeStruct((rows, cols), F32),
        [],
        6 * rows * cols * rank,
    )(o, rs, raw)


def last_raw_kernel(p_ref, rs_ref, w_ref, x_ref, raw_ref, o_ref, sq_ref):
    assemble_raw(w_ref, x_ref, raw_ref)
    raw = raw_ref[...]
    o_ref[...] = exact(p_ref[...] * rs_ref[:1], w_ref[...], NT)
    n = raw.shape[0]
    i = lax.broadcasted_iota(jnp.int32, (n, n), 0)
    j = lax.broadcasted_iota(jnp.int32, (n, n), 1)
    squares = jnp.where(i == j, jnp.broadcast_to(squares_of(raw), (n, n)), 0.0)
    row = jnp.sum(squares, axis=0, keepdims=True)
    for k in range(sq_ref.shape[0]):
        sq_ref[k] = jnp.broadcast_to(row, (8, n))


def last_raw(p, rs, w, x, peers):
    rows, rank = p.shape
    cols = x.shape[0] * LANES
    return call(
        last_raw_kernel,
        (1,),
        [whole(p.shape), whole(rs.shape), whole(w.shape), whole(x.shape)],
        [whole((rank, cols)), whole((rows, rank)), whole((peers, 8, rank))],
        [
            jax.ShapeDtypeStruct((rank, cols), F32),
            jax.ShapeDtypeStruct((rows, rank), F32),
            jax.ShapeDtypeStruct((peers, 8, rank), F32),
        ],
        [],
        3 * rows * cols * rank,
    )(p, rs, w, x)


def state_kernel(o_ref, raw_ref, b_ref, s_ref):
    o = split((1.0 - KEEP_RATE) * o_ref[...])
    s_ref[...] = b_ref[...] - dot3(o, split(raw_ref[...]), NN)


def last_state(o, raw, b):
    rows, cols = b.shape
    rank = o.shape[1]
    bn = cols // 4
    return call(
        state_kernel,
        (4,),
        [
            whole(o.shape),
            pl.BlockSpec((rank, bn), lambda i: (0, i)),
            pl.BlockSpec((rows, bn), lambda i: (0, i)),
        ],
        pl.BlockSpec((rows, bn), lambda i: (0, i)),
        jax.ShapeDtypeStruct((rows, cols), F32),
        [],
        6 * rows * cols * rank,
    )(o, raw, b)


def last_change_kernel(factor, o_ref, sq_ref, raw_ref, c_ref, out_ref):
    total = sq_ref[0, :1]
    for k in range(1, sq_ref.shape[0]):
        total = total + sq_ref[k, :1]
    o = split(o_ref[...] * (factor * lax.rsqrt(total + NORM_EPS)))
    out_ref[...] = (c_ref[...] + dot3(o, split(raw_ref[...]), NN)).astype(BF16)


def last_change(factor, o, sq, raw, change):
    rows, cols = change.shape
    rank = o.shape[1]
    bn = cols // 4
    return call(
        functools.partial(last_change_kernel, factor),
        (4,),
        [
            whole(o.shape),
            whole(sq.shape),
            pl.BlockSpec((rank, bn), lambda i: (0, i)),
            pl.BlockSpec((rows, bn), lambda i: (0, i)),
        ],
        pl.BlockSpec((rows, bn), lambda i: (0, i)),
        jax.ShapeDtypeStruct((rows, cols), BF16),
        [],
        6 * rows * cols * rank,
    )(o, sq, raw, change)


def exchange(x, axis, groups=None):
    return lax.all_to_all(x, axis, 0, 0, axis_index_groups=groups, tiled=True)


def copies(x, count):
    return jnp.broadcast_to(x[None], (count, *x.shape))


def col_sum(halves, axis):
    count = lax.axis_size(axis)
    swap = [(k, k ^ 1) for k in range(count)]
    even = [k for k in range(count) if k % 2 == 0]
    groups = [even, [k + 1 for k in even]]
    core = lax.axis_index(axis) % 2
    mine = lax.dynamic_index_in_dim(halves, core, 0, keepdims=False)
    theirs = lax.dynamic_index_in_dim(halves, 1 - core, 0, keepdims=False)
    mine = mine + lax.ppermute(theirs, axis, swap)
    mine = exchange(copies(mine, len(even)), axis, groups).sum(axis=0)
    theirs = lax.ppermute(mine, axis, swap)
    return jnp.where(core == 0, jnp.stack([mine, theirs]), jnp.stack([theirs, mine]))


def row_total(products, rank, axis):
    count = lax.axis_size(axis)
    own = exchange(products, axis).sum(axis=0)
    gram = exchange(copies(own[rank:], count), axis)
    raw = exchange(copies(own[:rank], count), axis)
    return gram, raw


def shards(momentum, grads, basis):
    rows, cols = momentum.shape
    rank = basis.shape[1]
    factor = (rows * lax.axis_size("row") * cols * lax.axis_size("col") / rank) ** 0.5

    p1 = first_projection(momentum, grads, basis)
    p1 = col_sum(p1.reshape(2, rows // 2, rank), "col").reshape(rows, rank)
    x1 = raw_products(
        raw_first_kernel,
        p1,
        [],
        [momentum, grads],
        lambda r, n: [
            pl.BlockSpec((r, n), lambda i: (0, i)),
            pl.BlockSpec((1, r, n), lambda i: (0, 0, i)),
        ],
        cols,
    )
    gram1, x1 = row_total(x1, rank, "row")
    w1 = inverse_factor(gram1)
    q2, raw1, o1 = middle(p1, w1, x1, momentum, grads)
    b2 = second_buffer(o1, raw1, momentum, grads)
    q2 = col_sum(q2, "col")
    p2 = q2[:, : rows // 2].reshape(rows, rank)
    rs1 = lax.rsqrt(q2[0, rows // 2 :] + NORM_EPS)
    x2 = raw_products(
        raw_second_kernel,
        p2,
        [rs1],
        [b2],
        lambda r, n: [pl.BlockSpec((r, n), lambda i: (0, i))],
        cols,
    )
    change1 = first_change(factor, o1, rs1, raw1)
    gram2, x2 = row_total(x2, rank, "row")
    w2 = inverse_factor(gram2)
    raw2, o2, sq2 = last_raw(p2, rs1, w2, x2, lax.axis_size("col"))
    sq2 = exchange(sq2, "col")
    state = last_state(o2, raw2, b2)
    change = last_change(factor, o2, sq2, raw2, change1)
    return change, state


def solution(mesh):
    return jax.shard_map(
        shards,
        mesh=mesh,
        in_specs=(P("row", "col"), P(None, "row", "col"), P("col", None)),
        out_specs=(P("row", "col"), P("row", "col")),
        check_vma=False,
    )
```

time: 476 us -> 273 us (0.57)
  other arithmetic: 119 us -> 3.47 us
  Pallas kernels: 0 us -> 97.4 us
  matrix products: 80.6 us -> 0 us
  waiting for transfers between devices: 87.2 us -> 19.5 us
  between operations: 17.3 us -> 0.87 us
  blocking collectives: 124 us -> 108 us
  local copies, waits for them, and re-layouts: 16.2 us -> 10.2 us
  starting transfers between devices: 27.2 us -> 32.4 us
    another operation x18 -> x0, other arithmetic: 109 us -> none  [the longest x13 68.7 us: shards(): lower = jnp.linalg.cholesky(gram)]
    pallas_call x0 -> x11, Pallas kernels: none -> 97.4 us  [the longest x2 46 us: inverse_factor(): call(cholesky_kernel, (1,), [whole(gram.shape)], whole((rank, rank)), jax...]
    dot_general x10 -> x0, matrix products: 75.5 us -> none  [the longest x2 23.1 us: shards(): jnp.dot(ortho, raw.T, precision=high, preferred_element_type=jnp.float32)]
    all_gather x2 -> x0, waiting for transfers between devices: 66.2 us -> none  [over_pieces(): parts = lax.all_gather(shard, axis)]
    all_to_all x6 -> x4, blocking collectives: 124 us -> 108 us  [exchange(): return lax.all_to_all(x, axis, 0, 0, axis_index_groups=groups, tiled=True)]
    ppermute x0 -> x4, starting transfers between devices: none -> 10.6 us  [the longest x2 7.11 us: col_sum(): mine = mine + lax.ppermute(theirs, axis, swap)]
    another operation x19 -> x0, local copies, waits for them, and re-layouts: 8.3 us -> none  [the longest x15 8.25 us: shards(): ortho = jax.scipy.linalg.solve_triangular(lower, projected.T, lower=True).T]
    reduce_sum x10 -> x4, other arithmetic: 10.8 us -> 3.33 us  [the longest x2 1.91 us: row_total(): own = exchange(products, axis).sum(axis=0)]
  transfers between devices with their start and end apart: 6 -> 9, of which waited for: 4 -> 6; matrix products, arithmetic and copies ran while one was open for 7% -> 0% of each run, Pallas kernels for 0% -> 23%
where the time goes in v1:
time: 273 us; the launch traced here: 272 us
  blocking collectives  108 us (40%)
  Pallas kernels  97.4 us (36%)
  starting transfers between devices  32.4 us (12%)
  waiting for transfers between devices  19.5 us (7%)
  local copies, waits for them, and re-layouts  10.2 us (4%)
  other arithmetic  3.47 us (1%)
    all_to_all x4, blocking collectives, exchange(): return lax.all_to_all(x, axis, 0, 0, axis_index_groups=groups, tiled=True)  108 us
    pallas_call x2, Pallas kernels, inverse_factor(): call(cholesky_kernel, (1,), [whole(gram.shape)], whole((rank, rank)), jax...  46 us
    all_to_all x5, starting transfers between devices, exchange(): return lax.all_to_all(x, axis, 0, 0, axis_index_groups=groups, tiled=True)  21.8 us
    all_to_all x5, waiting for transfers between devices, exchange(): return lax.all_to_all(x, axis, 0, 0, axis_index_groups=groups, tiled=True)  16 us
    pallas_call x2, Pallas kernels, raw_products(): call(functools.partial(kernel, blocks), (steps,), [whole(p.shape)] + [who...  11.3 us
    pallas_call x1, Pallas kernels, middle(): call(middle_kernel, (4,), [whole(p.shape), whole(w.shape), whole(x.shape)...  9.75 us
    ppermute x2, starting transfers between devices, col_sum(): mine = mine + lax.ppermute(theirs, axis, swap)  7.11 us
    pallas_call x1, Pallas kernels, second_buffer(): call(update_kernel, (4,), [whole(o.shape), pl.BlockSpec((rank, bn), lambd...  6.81 us
  transfers between devices with their start and end apart: 9, of which 6 were waited for; matrix products, arithmetic and copies ran while one was open for 0% of the time, Pallas kernels for 23%

profile of v1, /device:TPU:1, one launch (start us, length us, event | category | flops | bytes accessed | tf_op | source)
XLA Modules:
  0.0 272.1 jit_solution(15516649347499258000)
XLA Ops:
  0.7 1.6 copy-done.2
  2.2 4.9 %shard_map.50 = f32[512,256]{1,0:T(8,128)S(1)} custom-call(f32[512,2048]{1,0:T(8,128)} %m_ref.7, bf16[2,512,2048]{2,1,0:T(8,128)(2,1)} %g_ref.7, f32[2048,256]{1,0:T(8,128)S(1)} %copy-done.2), custom_call_target="tpu_custom_call" | custom-call | flops 1610612736 | bytes 8388608 | tf_op jit(solution)/shard_map/pallas_call | solution.py:72
  7.2 1.5 collective-permute-start
  8.7 1.2 collective-permute-done
  9.9 0.1 broadcast_in_dim.12
  10.0 18.1 %all_to_all.45 = f32[4,256,256]{2,1,0:T(8,128)S(1)} all-to-all(f32[4,256,256]{2,1,0:T(8,128)S(1)} %broadcast_in_dim.12), channel_id=1, replica_groups={{0,2,4,6},{1,3,5,7},{8,10,12,14},{9,11,13,15},{16,18,20,22},{17,19,21,2..., dimensions={0} | all-to-all | bytes 2097152 | tf_op jit(solution)/shard_map/all_to_all | solution.py:395
  28.1 0.1 reduce_sum.36
  28.2 1.9 collective-permute-start.1
  30.1 1.2 collective-permute-done.1
  31.3 5.9 %shard_map.51 = f32[16,288,128]{2,1,0:T(8,128)S(1)} custom-call(f32[512,256]{1,0:T(8,128)S(1)} %bitcast.17, f32[512,2048]{1,0:T(8,128)} %m_ref.7, bf16[2,512,2048]{2,1,0:T(8,128)(2,1)} %g_ref.7), custom_call_target="tpu_custom_call" | custom-call | flops 1610612736 | bytes 8388608 | tf_op jit(solution)/shard_map/pallas_call | solution.py:122
  37.3 37.7 %all_to_all.46 = f32[16,288,128]{2,1,0:T(8,128)S(1)} all-to-all(f32[16,288,128]{2,1,0:T(8,128)S(1)} %shard_map.51), channel_id=1, replica_groups=mesh['row'=16,'col'=8] {'row'}, dimensions={0} | all-to-all | bytes 4718592 | tf_op jit(solution)/shard_map/all_to_all | solution.py:395
  75.0 0.1 reduce_sum.37
  75.1 0.7 broadcast_in_dim.13
  75.8 3.6 %all-to-all-start.2 = ((f32[16,32,128]{2,1,0:T(8,128)}), f32[16,32,128]{2,1,0:T(8,128)S(1)}, u32[]{:S(2)}, u32[]{:S(2)}) async-start(f32[16,32,128]{2,1,0:T(8,128)} %broadcast_in_dim.13), calls=%async_computation.2 | async-start | bytes 524288 | tf_op jit(solution)/shard_map/all_to_all | solution.py:395
  79.5 7.3 %all-to-all-done.2.g_ref = f32[16,32,128]{2,1,0:T(8,128)S(1)} async-done(((f32[16,32,128]{2,1,0:T(8,128)}), f32[16,32,128]{2,1,0:T(8,128)S(1)}, u32[]{:S(2)}, u32[]{:S(2)}) %all-to-all-start.2) | async-done | bytes 262176 | tf_op jit(solution)/shard_map/all_to_all | solution.py:395
  86.8 1.5 broadcast_in_dim.14
  88.3 3.7 %all-to-all-start.3 = ((f32[16,256,128]{2,1,0:T(8,128)}), f32[16,256,128]{2,1,0:T(8,128)S(1)}, u32[]{:S(2)}, u32[]{:S(2)}) async-start(f32[16,256,128]{2,1,0:T(8,128)} %broadcast_in_dim.14), calls=%async_computation.3 | async-start | bytes 4194304 | tf_op jit(solution)/shard_map/all_to_all | solution.py:395
  92.0 23.0 %shard_map.52.w_ref = f32[256,256]{1,0:T(8,128)S(1)} custom-call(f32[16,32,128]{2,1,0:T(8,128)S(1)} %all-to-all-done.2.g_ref), custom_call_target="tpu_custom_call" | custom-call | flops 10000000000 | bytes 8388608 | tf_op jit(solution)/shard_map/pallas_call | solution.py:189
  115.0 2.3 all-to-all-done.3.x_ref
  117.3 9.8 %shard_map.53 = (f32[2,264,256]{2,1,0:T(8,128)S(1)}, f32[256,2048]{1,0:T(8,128)S(1)}, f32[512,256]{1,0:T(8,128)S(1)}) custom-call(f32[512,256]{1,0:T(8,128)S(1)} %bitcast.18, f32[256,256]{1,0:T(8,128)S(1)} %shard_map.52.w_ref, f32[16,256,128]{2,1,0:T(8,128)S(1)} %all-to-all-done.3.x_ref, f32[512,2048]{1,0:T(8,128)} %m_ref.7, bf16[2,512,2048]{2,1,0:T(8,128)(2,1)} %g_ref.7), custom_call_target="tpu_custom_call" | custom-call | flops 2684354560 | bytes 8388608 | tf_op jit(solution)/shard_map/pallas_call | solution.py:244
  127.1 0.0 copy-start
  127.1 1.3 copy-done
  128.4 5.6 %collective-permute-start.2 = (f32[264,256]{1,0:T(8,128)S(1)}, f32[264,256]{1,0:T(8,128)S(1)}, u32[]{:S(2)}, u32[]{:S(2)}) collective-permute-start(f32[264,256]{1,0:T(8,128)S(1)} %dynamic-slice_bitcast_fusion), channel_id=1, source_target_pairs={{0,1},{1,0},{2,3},{3,2},{4,5},{5,4},{6,7},{7,6},{8,9},{9,8},{10,11... | collective-permute-start | bytes 811016 | tf_op jit(solution)/shard_map/ppermute | solution.py:410
  134.0 1.2 collective-permute-done.2
  135.2 0.1 broadcast_in_dim.15
  135.3 0.0 copy-start.1
  135.3 18.3 %all_to_all.47 = f32[4,264,256]{2,1,0:T(8,128)} all-to-all(f32[4,264,256]{2,1,0:T(8,128)S(1)} %broadcast_in_dim.15), channel_id=1, replica_groups={{0,2,4,6},{1,3,5,7},{8,10,12,14},{9,11,13,15},{16,18,20,22},{17,19,21,2..., dimensions={0} | all-to-all | bytes 2162688 | tf_op jit(solution)/shard_map/all_to_all | solution.py:395
  153.7 1.3 reduce_sum.38
  155.0 1.6 collective-permute-start.3
  156.6 6.8 %shard_map.54.b_ref = f32[512,2048]{1,0:T(8,128)} custom-call(f32[512,256]{1,0:T(8,128)S(1)} %get-tuple-element.9.o_ref, f32[256,2048]{1,0:T(8,128)S(1)} %copy-done.1, f32[512,2048]{1,0:T(8,128)} %m_ref.7, bf16[2,512,2048]{2,1,0:T(8,128)(2,1)} %g_ref.7), custom_call_target="tpu_custom_call" | custom-call | flops 1610612736 | bytes 8388608 | tf_op jit(solution)/shard_map/pallas_call | solution.py:275
  163.5 5.4 %shard_map.55 = f32[16,288,128]{2,1,0:T(8,128)S(1)} custom-call(f32[512,256]{1,0:T(8,128)S(1)} %bitcast.19, f32[8,256]{1,0:T(8,128)S(1)} %fusion.1.rs_ref, f32[512,2048]{1,0:T(8,128)} %shard_map.54.b_ref), custom_call_target="tpu_custom_call" | custom-call | flops 1610612736 | bytes 8388608 | tf_op jit(solution)/shard_map/pallas_call | solution.py:122
  168.9 34.0 %all_to_all.48 = f32[16,288,128]{2,1,0:T(8,128)} all-to-all(f32[16,288,128]{2,1,0:T(8,128)S(1)} %shard_map.55), channel_id=1, replica_groups=mesh['row'=16,'col'=8] {'row'}, dimensions={0} | all-to-all | bytes 4718592 | tf_op jit(solution)/shard_map/all_to_all | solution.py:395
  202.9 1.8 reduce_sum.39
  204.7 0.0 copy-start.5
  204.7 0.7 broadcast_in_dim.16
  205.5 3.8 %all-to-all-start.6 = ((f32[16,32,128]{2,1,0:T(8,128)}), f32[16,32,128]{2,1,0:T(8,128)S(1)}, u32[]{:S(2)}, u32[]{:S(2)}) async-start(f32[16,32,128]{2,1,0:T(8,128)} %broadcast_in_dim.16), calls=%async_computation.6 | async-start | bytes 524288 | tf_op jit(solution)/shard_map/all_to_all | solution.py:395
  209.3 0.9 slice.29
  210.2 6.4 %all-to-all-done.6.g_ref = f32[16,32,128]{2,1,0:T(8,128)S(1)} async-done(((f32[16,32,128]{2,1,0:T(8,128)}), f32[16,32,128]{2,1,0:T(8,128)S(1)}, u32[]{:S(2)}, u32[]{:S(2)}) %all-to-all-start.6) | async-done | bytes 262176 | tf_op jit(solution)/shard_map/all_to_all | solution.py:395
  216.6 1.5 broadcast_in_dim.17
  218.2 4.4 %all-to-all-start.7 = ((f32[16,256,128]{2,1,0:T(8,128)}), f32[16,256,128]{2,1,0:T(8,128)}, u32[]{:S(2)}, u32[]{:S(2)}) async-start(f32[16,256,128]{2,1,0:T(8,128)} %broadcast_in_dim.17), calls=%async_computation.7 | async-start | bytes 4194304 | tf_op jit(solution)/shard_map/all_to_all | solution.py:395
  222.6 4.1 %shard_map.58.c_ref = f32[512,2048]{1,0:T(8,128)} custom-call(f32[512,256]{1,0:T(8,128)S(1)} %get-tuple-element.9.o_ref, f32[8,256]{1,0:T(8,128)S(1)} %fusion.1.rs_ref, f32[256,2048]{1,0:T(8,128)S(1)} %copy-done.1), custom_call_target="tpu_custom_call" | custom-call | flops 1610612736 | bytes 8388608 | tf_op jit(solution)/shard_map/pallas_call | solution.py:300
  226.7 23.0 %shard_map.56.w_ref = f32[256,256]{1,0:T(8,128)S(1)} custom-call(f32[16,32,128]{2,1,0:T(8,128)S(1)} %all-to-all-done.6.g_ref), custom_call_target="tpu_custom_call" | custom-call | flops 10000000000 | bytes 8388608 | tf_op jit(solution)/shard_map/pallas_call | solution.py:189
  249.7 0.7 copy-done.3
  250.4 0.9 copy-done.4
  251.3 3.4 %shard_map.57 = (f32[256,2048]{1,0:T(8,128)S(1)}, f32[512,256]{1,0:T(8,128)S(1)}, f32[8,8,256]{2,1,0:T(8,128)}) custom-call(f32[512,256]{1,0:T(8,128)S(1)} %bitcast.20, f32[8,256]{1,0:T(8,128)S(1)} %fusion.1.rs_ref, f32[256,256]{1,0:T(8,128)S(1)} %copy-done.4, f32[16,256,128]{2,1,0:T(8,128)} %all-to-all-done.7.x_ref), custom_call_target="tpu_custom_call" | custom-call | flops 805306368 | bytes 8388608 | tf_op jit(solution)/shard_map/pallas_call | solution.py:327
  254.7 6.2 %all-to-all-start.8 = ((f32[8,8,256]{2,1,0:T(8,128)}), f32[8,8,256]{2,1,0:T(8,128)S(1)}, u32[]{:S(2)}, u32[]{:S(2)}) async-start(f32[8,8,256]{2,1,0:T(8,128)} %get-tuple-element.12), calls=%async_computation.8 | async-start | bytes 131072 | tf_op jit(solution)/shard_map/all_to_all | solution.py:395
  260.9 5.8 %shard_map.60 = f32[512,2048]{1,0:T(8,128)} custom-call(f32[512,256]{1,0:T(8,128)S(1)} %get-tuple-element.11.o_ref, f32[256,2048]{1,0:T(8,128)S(1)} %get-tuple-element.13.raw_ref, f32[512,2048]{1,0:T(8,128)} %shard_map.54.b_ref), custom_call_target="tpu_custom_call" | custom-call | flops 1610612736 | bytes 8388608 | tf_op jit(solution)/shard_map/pallas_call | solution.py:351
  266.7 5.4 %shard_map.59 = bf16[512,2048]{1,0:T(8,128)(2,1)} custom-call(f32[512,256]{1,0:T(8,128)S(1)} %get-tuple-element.11.o_ref, f32[8,8,256]{2,1,0:T(8,128)S(1)} %all-to-all-done.8.sq_ref, f32[256,2048]{1,0:T(8,128)S(1)} %get-tuple-element.13.raw_ref, f32[512,2048]{1,0:T(8,128)} %shard_map.58.c_ref), custom_call_target="tpu_custom_call" | custom-call | flops 1610612736 | bytes 8388608 | tf_op jit(solution)/shard_map/pallas_call | solution.py:378
  (19 shorter events, 0.3 us)
Async XLA Ops:
  0.6 1.6 copy-start.2
  7.2 2.7 collective-permute-start
  28.2 3.1 %collective-permute-start.1 = (f32[256,256]{1,0:T(8,128)S(1)}, f32[256,256]{1,0:T(8,128)S(1)}, u32[]{:S(2)}, u32[]{:S(2)}) collective-permute-start(f32[256,256]{1,0:T(8,128)S(1)} %reduce_sum.36), channel_id=1, source_target_pairs={{0,1},{1,0},{2,3},{3,2},{4,5},{5,4},{6,7},{7,6},{8,9},{9,8},{10,11... | collective-permute-start | bytes 786440 | tf_op jit(solution)/shard_map/ppermute | solution.py:412
  75.8 10.9 %all-to-all-start.2 = ((f32[16,32,128]{2,1,0:T(8,128)}), f32[16,32,128]{2,1,0:T(8,128)S(1)}, u32[]{:S(2)}, u32[]{:S(2)}) async-start(f32[16,32,128]{2,1,0:T(8,128)} %broadcast_in_dim.13), calls=%async_computation.2 | async-start | bytes 524288 | tf_op jit(solution)/shard_map/all_to_all | solution.py:395
  88.3 29.0 %all-to-all-start.3 = ((f32[16,256,128]{2,1,0:T(8,128)}), f32[16,256,128]{2,1,0:T(8,128)S(1)}, u32[]{:S(2)}, u32[]{:S(2)}) async-start(f32[16,256,128]{2,1,0:T(8,128)} %broadcast_in_dim.14), calls=%async_computation.3 | async-start | bytes 4194304 | tf_op jit(solution)/shard_map/all_to_all | solution.py:395
  127.1 1.3 copy-start
  128.4 6.8 %collective-permute-start.2 = (f32[264,256]{1,0:T(8,128)S(1)}, f32[264,256]{1,0:T(8,128)S(1)}, u32[]{:S(2)}, u32[]{:S(2)}) collective-permute-start(f32[264,256]{1,0:T(8,128)S(1)} %dynamic-slice_bitcast_fusion), channel_id=1, source_target_pairs={{0,1},{1,0},{2,3},{3,2},{4,5},{5,4},{6,7},{7,6},{8,9},{9,8},{10,11... | collective-permute-start | bytes 811016 | tf_op jit(solution)/shard_map/ppermute | solution.py:410
  135.3 21.3 %copy-start.1 = (f32[256,2048]{1,0:T(8,128)S(1)}, f32[256,2048]{1,0:T(8,128)}, u32[]{:S(2)}) copy-start(f32[256,2048]{1,0:T(8,128)} %copy-done) | copy-start | bytes 6291460
  155.0 8.4 %collective-permute-start.3 = (f32[264,256]{1,0:T(8,128)S(1)}, f32[264,256]{1,0:T(8,128)S(1)}, u32[]{:S(2)}, u32[]{:S(2)}) collective-permute-start(f32[264,256]{1,0:T(8,128)S(1)} %reduce_sum.38), channel_id=1, source_target_pairs={{0,1},{1,0},{2,3},{3,2},{4,5},{5,4},{6,7},{7,6},{8,9},{9,8},{10,11... | collective-permute-start | bytes 811016 | tf_op jit(solution)/shard_map/ppermute | solution.py:412
  204.7 0.8 copy-start.5
  205.5 11.2 %all-to-all-start.6 = ((f32[16,32,128]{2,1,0:T(8,128)}), f32[16,32,128]{2,1,0:T(8,128)S(1)}, u32[]{:S(2)}, u32[]{:S(2)}) async-start(f32[16,32,128]{2,1,0:T(8,128)} %broadcast_in_dim.16), calls=%async_computation.6 | async-start | bytes 524288 | tf_op jit(solution)/shard_map/all_to_all | solution.py:395
  218.2 32.2 %all-to-all-start.7 = ((f32[16,256,128]{2,1,0:T(8,128)}), f32[16,256,128]{2,1,0:T(8,128)}, u32[]{:S(2)}, u32[]{:S(2)}) async-start(f32[16,256,128]{2,1,0:T(8,128)} %broadcast_in_dim.17), calls=%async_computation.7 | async-start | bytes 4194304 | tf_op jit(solution)/shard_map/all_to_all | solution.py:395
  249.7 0.7 copy-start.3
  250.4 1.0 copy-start.4
  254.7 12.0 %all-to-all-start.8 = ((f32[8,8,256]{2,1,0:T(8,128)}), f32[8,8,256]{2,1,0:T(8,128)S(1)}, u32[]{:S(2)}, u32[]{:S(2)}) async-start(f32[8,8,256]{2,1,0:T(8,128)} %get-tuple-element.12), calls=%async_computation.8 | async-start | bytes 131072 | tf_op jit(solution)/shard_map/all_to_all | solution.py:395

commit v2 on v1

v2 whole, which is shorter than its diff:
```python
import functools

import jax
import jax.numpy as jnp
from jax import lax
from jax.experimental import pallas as pl
from jax.experimental.pallas import tpu as pltpu
from jax.sharding import PartitionSpec as P

KEEP_RATE = 0.95
NORM_EPS = 1e-06
LANES = 128
GRID = 4
F32 = jnp.float32
BF16 = jnp.bfloat16
VMEM_LIMIT = 48 * 1024 * 1024
NN = (((1,), (0,)), ((), ()))
NT = (((1,), (1,)), ((), ()))


def split(x):
    high = x.astype(BF16)
    return high, (x - high.astype(F32)).astype(BF16)


def mm(a, b, dims):
    return lax.dot_general(a, b, dims, preferred_element_type=F32)


def dot3(a, b, dims):
    return mm(a[0], b[0], dims) + (mm(a[0], b[1], dims) + mm(a[1], b[0], dims))


def exact(a, b, dims):
    return lax.dot_general(
        a, b, dims, precision=lax.Precision.HIGHEST, preferred_element_type=F32
    )


def call(kernel, grid, in_specs, out_specs, out_shape, scratch, cost):
    return pl.pallas_call(
        kernel,
        grid=grid,
        in_specs=in_specs,
        out_specs=out_specs,
        out_shape=out_shape,
        scratch_shapes=scratch,
        compiler_params=pltpu.CompilerParams(vmem_limit_bytes=VMEM_LIMIT),
        cost_estimate=pl.CostEstimate(
            flops=cost, transcendentals=0, bytes_accessed=8 * 1024 * 1024
        ),
    )


def whole(shape):
    return pl.BlockSpec(shape, lambda i: (0,) * len(shape))


def first_kernel(m_ref, g_ref, v_ref, p_ref):
    b = split(m_ref[...] + g_ref[0].astype(F32))
    part = dot3(b, split(v_ref[...]), NN)

    @pl.when(pl.program_id(0) == 0)
    def _():
        p_ref[...] = part

    @pl.when(pl.program_id(0) > 0)
    def _():
        p_ref[...] += part


def first_projection(momentum, grads, basis):
    rows, cols = momentum.shape
    rank = basis.shape[1]
    bn = cols // GRID
    return call(
        first_kernel,
        (GRID,),
        [
            pl.BlockSpec((rows, bn), lambda i: (0, i)),
            pl.BlockSpec((1, rows, bn), lambda i: (0, 0, i)),
            pl.BlockSpec((bn, rank), lambda i: (i, 0)),
        ],
        whole((rows, rank)),
        jax.ShapeDtypeStruct((rows, rank), F32),
        [],
        6 * rows * cols * rank,
    )(momentum, grads, basis)


def gram_kernel(n_ref, p_ref, pt_ref, c_ref, scratch):
    turned = p_ref[...].T
    scratch[...] = turned
    pt_ref[0], pt_ref[1] = split(turned)
    size = c_ref.shape[0]
    first = pl.multiple_of(n_ref[0] * size, size)
    c_ref[...] = exact(scratch[pl.ds(first, size), :], p_ref[...], NN)


def gram_part(p, index, parts):
    rows, rank = p.shape
    return call(
        gram_kernel,
        (1,),
        [pl.BlockSpec(memory_space=pltpu.SMEM), whole(p.shape)],
        [whole((2, rank, rows)), whole((rank // parts, rank))],
        [
            jax.ShapeDtypeStruct((2, rank, rows), BF16),
            jax.ShapeDtypeStruct((rank // parts, rank), F32),
        ],
        [pltpu.VMEM((rank, rows), F32)],
        2 * rows * rank * rank,
    )(index, p)


def store_products(pt_ref, b, x_ref):
    r = dot3((pt_ref[0], pt_ref[1]), split(b), NN)
    for k in range(x_ref.shape[0]):
        x_ref[k] = r[:, k * LANES : (k + 1) * LANES]


def raw_first_kernel(pt_ref, m_ref, g_ref, x_ref):
    store_products(pt_ref, m_ref[...] + g_ref[0].astype(F32), x_ref)


def raw_second_kernel(pt_ref, b_ref, x_ref):
    store_products(pt_ref, b_ref[...], x_ref)


def raw_products(kernel, pt, bigs):
    _, rank, rows = pt.shape
    cols = bigs[0].shape[1]
    bn = cols // GRID
    specs = [
        pl.BlockSpec((rows, bn), lambda i: (0, i)),
        pl.BlockSpec((1, rows, bn), lambda i: (0, 0, i)),
    ]
    return call(
        kernel,
        (GRID,),
        [whole(pt.shape)] + specs[: len(bigs)],
        pl.BlockSpec((bn // LANES, rank, LANES), lambda i: (i, 0, 0)),
        jax.ShapeDtypeStruct((cols // LANES, rank, LANES), F32),
        [],
        6 * rows * cols * rank,
    )(pt, *bigs)


def spread_kernel(x_ref, y_ref):
    count = x_ref.shape[0]
    total = x_ref[0]
    for k in range(1, count):
        total = total + x_ref[k]
    for k in range(count):
        y_ref[k] = total


def spread_sum(x):
    count, height, width = x.shape
    spec = pl.BlockSpec((count, height // 4, width), lambda i: (0, i, 0))
    return call(
        spread_kernel, (4,), [spec], spec, jax.ShapeDtypeStruct(x.shape, F32), [], count * height * width
    )(x)


def eliminated(m):
    n = m.shape[0]
    lane = lax.broadcasted_iota(jnp.int32, (8, n), 1)
    sub = lax.broadcasted_iota(jnp.int32, (8, n), 0)
    tiles = [m[8 * t : 8 * t + 8] for t in range(n // 8)]
    for j in range(n):
        t, r = divmod(j, 8)
        row = tiles[t][r : r + 1]
        inv = 1.0 / row[:, j : j + 1]
        here = lane == j
        scaled = jnp.where(here[:1], inv, row * inv)
        for s in range(t, n // 8):
            column = jnp.broadcast_to(tiles[s][:, j : j + 1], (8, n))
            new = jnp.where(here, 0.0, tiles[s]) - column * scaled
            if s == t:
                new = jnp.where(sub > r, new, tiles[s])
            tiles[s] = new
    m = jnp.concatenate(tiles, axis=0)
    i = lax.broadcasted_iota(jnp.int32, (n, n), 0)
    j = lax.broadcasted_iota(jnp.int32, (n, n), 1)
    pivots = jnp.sum(jnp.where(i == j, m, 0.0), axis=1, keepdims=True)
    unit = jnp.where(i > j, m, jnp.where(i == j, 1.0, 0.0))
    return unit * lax.rsqrt(pivots)


def cholesky_kernel(n_ref, *refs):
    pieces, (w_ref, a, low) = refs[:-3], refs[-3:]
    size = pieces[0].shape[0]
    count = len(pieces)
    for k, piece in enumerate(pieces):
        place = lax.rem(n_ref[0] + k, count)
        a[pl.ds(pl.multiple_of(place * size, size), size), :] = piece[...]
    half = LANES

    def body(b, carry):
        first = pl.multiple_of(b * half, half)
        w = eliminated(a[pl.ds(first, half), pl.ds(first, half)])
        w_ref[pl.ds(first, half), pl.ds(first, half)] = w

        @pl.when(b == 0)
        def _():
            low[...] = exact(a[half:, :half], w, NT)
            a[half:, half:] -= exact(low[...], low[...], NT)

        return carry

    lax.fori_loop(0, 2, body, 0)
    w_ref[:half, half:] = jnp.zeros((half, half), F32)
    w_ref[half:, :half] = -exact(
        w_ref[half:, half:], exact(low[...], w_ref[:half, :half], NN), NN
    )


def inverse_factor(pieces, index):
    rank = pieces[0].shape[1]
    return call(
        cholesky_kernel,
        (1,),
        [pl.BlockSpec(memory_space=pltpu.SMEM)] + [whole(q.shape) for q in pieces],
        whole((rank, rank)),
        jax.ShapeDtypeStruct((rank, rank), F32),
        [pltpu.VMEM((rank, rank), F32), pltpu.VMEM((LANES, LANES), F32)],
        10**10,
    )(index, *pieces)


def joined(x_ref):
    return jnp.concatenate([x_ref[k] for k in range(x_ref.shape[0])], axis=1)


def same(n):
    i = lax.broadcasted_iota(jnp.int32, (n, n), 0)
    return i == lax.broadcasted_iota(jnp.int32, (n, n), 1)


def middle_kernel(p_ref, w_ref, x_ref, m_ref, g_ref, q_ref, o_ref, q_sum, s_sum):
    step = pl.program_id(0)

    @pl.when(step == 0)
    def _():
        q_sum[...] = jnp.zeros_like(q_sum)
        s_sum[...] = jnp.zeros_like(s_sum)
        o_ref[...] = exact(p_ref[...], w_ref[...], NT)

    rt = split(joined(x_ref))
    b = m_ref[...] + g_ref[0].astype(F32) + g_ref[1].astype(F32)
    q_sum[...] += dot3(split(b), rt, NT)
    s_sum[...] += dot3(rt, rt, NT)

    @pl.when(step == pl.num_programs(0) - 1)
    def _():
        w = w_ref[...]
        s = exact(exact(w, s_sum[...], NN), w, NT)
        o = split((1.0 - KEEP_RATE) * o_ref[...])
        q = dot3(split(q_sum[...]), split(w), NT) - dot3(o, split(s), NN)
        n = s.shape[0]
        squares = jnp.sum(jnp.where(same(n), s, 0.0), axis=0, keepdims=True)
        height = q_ref.shape[1] - 8
        for k in range(q_ref.shape[0]):
            q_ref[k, :height] = q[k * height : (k + 1) * height]
            q_ref[k, height:] = jnp.broadcast_to(squares, (8, n))


def middle(p, w, x, momentum, grads):
    rows, cols = momentum.shape
    rank = p.shape[1]
    bn = cols // GRID
    shape = (4, rows // 4 + 8, rank)
    return call(
        middle_kernel,
        (GRID,),
        [
            whole(p.shape),
            whole(w.shape),
            pl.BlockSpec((bn // LANES, rank, LANES), lambda i: (i, 0, 0)),
            pl.BlockSpec((rows, bn), lambda i: (0, i)),
            pl.BlockSpec((2, rows, bn), lambda i: (0, 0, i)),
        ],
        [whole(shape), whole((rows, rank))],
        [jax.ShapeDtypeStruct(shape, F32), jax.ShapeDtypeStruct((rows, rank), F32)],
        [pltpu.VMEM((rows, rank), F32), pltpu.VMEM((rank, rank), F32)],
        10 * rows * cols * rank,
    )(p, w, x, momentum, grads)


def update_kernel(o_ref, w_ref, x_ref, m_ref, g_ref, raw_ref, b_ref):
    raw = dot3(split(w_ref[...]), split(joined(x_ref)), NN)
    raw_ref[...] = raw
    b = m_ref[...] + g_ref[0].astype(F32) + g_ref[1].astype(F32)
    o = split((1.0 - KEEP_RATE) * o_ref[...])
    b_ref[...] = b - dot3(o, split(raw), NN)


def second_buffer(o, w, x, momentum, grads):
    rows, cols = momentum.shape
    rank = o.shape[1]
    bn = cols // GRID
    return call(
        update_kernel,
        (GRID,),
        [
            whole(o.shape),
            whole(w.shape),
            pl.BlockSpec((bn // LANES, rank, LANES), lambda i: (i, 0, 0)),
            pl.BlockSpec((rows, bn), lambda i: (0, i)),
            pl.BlockSpec((2, rows, bn), lambda i: (0, 0, i)),
        ],
        [
            pl.BlockSpec((rank, bn), lambda i: (0, i)),
            pl.BlockSpec((rows, bn), lambda i: (0, i)),
        ],
        [
            jax.ShapeDtypeStruct((rank, cols), F32),
            jax.ShapeDtypeStruct((rows, cols), F32),
        ],
        [],
        9 * rows * cols * rank,
    )(o, w, x, momentum, grads)


def change_kernel(factor, o_ref, rs_ref, raw_ref, c_ref):
    o = split(o_ref[...] * (factor * rs_ref[:1]))
    c_ref[...] = dot3(o, split(raw_ref[...]), NN)


def first_change(factor, o, rs, raw):
    rows, rank = o.shape
    cols = raw.shape[1]
    bn = cols // GRID
    return call(
        functools.partial(change_kernel, factor),
        (GRID,),
        [whole(o.shape), whole(rs.shape), pl.BlockSpec((rank, bn), lambda i: (0, i))],
        pl.BlockSpec((rows, bn), lambda i: (0, i)),
        jax.ShapeDtypeStruct((rows, cols), F32),
        [],
        6 * rows * cols * rank,
    )(o, rs, raw)


def last_raw_kernel(p_ref, w_ref, x_ref, raw_ref, o_ref, sq_ref, total):
    step = pl.program_id(0)

    @pl.when(step == 0)
    def _():
        o_ref[...] = exact(p_ref[...], w_ref[...], NT)
        total[...] = jnp.zeros_like(total)

    raw = dot3(split(w_ref[...]), split(joined(x_ref)), NN)
    raw_ref[...] = raw
    total[...] += jnp.sum(raw * raw, axis=1, keepdims=True)

    @pl.when(step == pl.num_programs(0) - 1)
    def _():
        n = raw.shape[0]
        squares = jnp.where(same(n), jnp.broadcast_to(total[:, :1], (n, n)), 0.0)
        row = jnp.sum(squares, axis=0, keepdims=True)
        for k in range(sq_ref.shape[0]):
            sq_ref[k] = jnp.broadcast_to(row, (8, n))


def last_raw(p, w, x, peers):
    rows, rank = p.shape
    cols = x.shape[0] * LANES
    bn = cols // GRID
    return call(
        last_raw_kernel,
        (GRID,),
        [
            whole(p.shape),
            whole(w.shape),
            pl.BlockSpec((bn // LANES, rank, LANES), lambda i: (i, 0, 0)),
        ],
        [
            pl.BlockSpec((rank, bn), lambda i: (0, i)),
            whole((rows, rank)),
            whole((peers, 8, rank)),
        ],
        [
            jax.ShapeDtypeStruct((rank, cols), F32),
            jax.ShapeDtypeStruct((rows, rank), F32),
            jax.ShapeDtypeStruct((peers, 8, rank), F32),
        ],
        [pltpu.VMEM((rank, LANES), F32)],
        3 * rows * cols * rank,
    )(p, w, x)


def state_kernel(o_ref, raw_ref, b_ref, s_ref):
    o = split((1.0 - KEEP_RATE) * o_ref[...])
    s_ref[...] = b_ref[...] - dot3(o, split(raw_ref[...]), NN)


def last_state(o, raw, b):
    rows, cols = b.shape
    rank = o.shape[1]
    bn = cols // GRID
    return call(
        state_kernel,
        (GRID,),
        [
            whole(o.shape),
            pl.BlockSpec((rank, bn), lambda i: (0, i)),
            pl.BlockSpec((rows, bn), lambda i: (0, i)),
        ],
        pl.BlockSpec((rows, bn), lambda i: (0, i)),
        jax.ShapeDtypeStruct((rows, cols), F32),
        [],
        6 * rows * cols * rank,
    )(o, raw, b)


def last_change_kernel(factor, o_ref, sq_ref, raw_ref, c_ref, out_ref):
    total = sq_ref[0, :1]
    for k in range(1, sq_ref.shape[0]):
        total = total + sq_ref[k, :1]
    o = split(o_ref[...] * (factor * lax.rsqrt(total + NORM_EPS)))
    out_ref[...] = (c_ref[...] + dot3(o, split(raw_ref[...]), NN)).astype(BF16)


def last_change(factor, o, sq, raw, change):
    rows, cols = change.shape
    rank = o.shape[1]
    bn = cols // GRID
    return call(
        functools.partial(last_change_kernel, factor),
        (GRID,),
        [
            whole(o.shape),
            whole(sq.shape),
            pl.BlockSpec((rank, bn), lambda i: (0, i)),
            pl.BlockSpec((rows, bn), lambda i: (0, i)),
        ],
        pl.BlockSpec((rows, bn), lambda i: (0, i)),
        jax.ShapeDtypeStruct((rows, cols), BF16),
        [],
        6 * rows * cols * rank,
    )(o, sq, raw, change)


SIDE = 4


def row_permute(x, move):
    pairs = []
    for y in range(SIDE):
        for z in range(SIDE):
            to = move(y, z)
            pairs.append((SIDE * y + z, SIDE * to[0] + to[1]))
    return lax.ppermute(x, "row", pairs)


def chip_permute(x, move):
    pairs = [(2 * k + c, 2 * move(k) + c) for k in range(SIDE) for c in range(2)]
    return lax.ppermute(x, "col", pairs)


def core_permute(x):
    return lax.ppermute(x, "col", [(k, k ^ 1) for k in range(2 * SIDE)])


def near(k):
    return k ^ 1


def far(k):
    return SIDE - 1 - k


def col_sum(parts):
    core = lax.axis_index("col") % 2
    mine = lax.dynamic_slice_in_dim(parts, 2 * core, 2, 0)
    theirs = lax.dynamic_slice_in_dim(parts, 2 - 2 * core, 2, 0)
    mine = mine + core_permute(theirs)
    a, b = mine[0], mine[1]
    a, b = a + chip_permute(a, near), b + chip_permute(b, far)
    a, b = a + chip_permute(a, far), b + chip_permute(b, near)
    mine = jnp.stack([a, b])
    theirs = core_permute(mine)
    return jnp.where(
        core == 0, jnp.concatenate([mine, theirs]), jnp.concatenate([theirs, mine])
    )


def gram_sum(part):
    for move in (
        lambda y, z: (y, near(z)),
        lambda y, z: (y, far(z)),
        lambda y, z: (near(y), z),
        lambda y, z: (far(y), z),
    ):
        part = part + row_permute(part, move)
    core = lax.axis_index("col") % 2
    other = core_permute(part)
    chip = jnp.where(
        core == 0, jnp.concatenate([part, other]), jnp.concatenate([other, part])
    )
    return [chip] + [
        chip_permute(chip, lambda k, d=d: (k - d) % SIDE) for d in range(1, SIDE)
    ]


def exchange(x, axis):
    return lax.all_to_all(x, axis, 0, 0, tiled=True)


def row_total(products, part, chip):
    pieces = gram_sum(part)
    own = spread_sum(exchange(products, "row"))
    pieces, own = lax.optimization_barrier((pieces, own))
    total = exchange(own, "row")
    return total, inverse_factor(pieces, chip)


def shards(momentum, grads, basis):
    rows, cols = momentum.shape
    rank = basis.shape[1]
    peers = lax.axis_size("col")
    factor = (rows * lax.axis_size("row") * cols * peers / rank) ** 0.5
    place = lax.axis_index("col").astype(jnp.int32)
    chip, place = (place // 2)[None], place[None]

    p1 = first_projection(momentum, grads, basis)
    p1 = col_sum(p1.reshape(4, rows // 4, rank)).reshape(rows, rank)
    pt1, part1 = gram_part(p1, place, peers)
    x1 = raw_products(raw_first_kernel, pt1, [momentum, grads])
    x1, w1 = row_total(x1, part1, chip)
    q2, o1 = middle(p1, w1, x1, momentum, grads)
    raw1, b2 = second_buffer(o1, w1, x1, momentum, grads)
    q2 = col_sum(q2)
    rs1 = lax.rsqrt(q2[0, rows // 4 :] + NORM_EPS)
    p2 = q2[:, : rows // 4].reshape(rows, rank) * rs1[:1]
    pt2, part2 = gram_part(p2, place, peers)
    x2 = raw_products(raw_second_kernel, pt2, [b2])
    change1 = first_change(factor, o1, rs1, raw1)
    x2, w2 = row_total(x2, part2, chip)
    raw2, o2, sq2 = last_raw(p2, w2, x2, peers)
    sq2 = exchange(sq2, "col")
    state = last_state(o2, raw2, b2)
    change = last_change(factor, o2, sq2, raw2, change1)
    return change, state


def solution(mesh):
    return jax.shard_map(
        shards,
        mesh=mesh,
        in_specs=(P("row", "col"), P(None, "row", "col"), P("col", None)),
        out_specs=(P("row", "col"), P("row", "col")),
        check_vma=False,
    )
```

time: 273 us -> 276 us (1.011)
  blocking collectives: 108 us -> 0 us
  starting transfers between devices: 32.4 us -> 102 us
  waiting for transfers between devices: 19.5 us -> 60.7 us
  local copies, waits for them, and re-layouts: 10.2 us -> 14.3 us
  other arithmetic: 3.47 us -> 0.47 us
    all_to_all x4 -> x0, blocking collectives: 108 us -> none  [exchange(): return lax.all_to_all(x, axis, 0, 0, axis_index_groups=groups, tiled=True)]
    ppermute x4 -> x28, starting transfers between devices: 10.6 us -> 76.9 us  [the longest x8 42.5 us: row_permute(): return lax.ppermute(x, 'row', pairs)]
    ppermute x4 -> x28, waiting for transfers between devices: 3.5 us -> 58.2 us  [the longest x8 30.4 us: row_permute(): return lax.ppermute(x, 'row', pairs)]
    all_to_all x5, waiting for transfers between devices: 16 us -> 2.52 us  [exchange(): return lax.all_to_all(x, axis, 0, 0, tiled=True)]
    unnamed x12 -> x22, local copies, waits for them, and re-layouts: 4.56 us -> 14.2 us
    broadcast_in_dim x6 -> x0, local copies, waits for them, and re-layouts: 4.65 us -> none  [copies(): return jnp.broadcast_to(x[None], (count, *x.shape))]
    reduce_sum x4 -> x0, other arithmetic: 3.33 us -> none  [the longest x2 1.91 us: row_total(): own = exchange(products, axis).sum(axis=0)]
    all_to_all x5, starting transfers between devices: 21.8 us -> 25 us  [exchange(): return lax.all_to_all(x, axis, 0, 0, tiled=True)]
  transfers between devices with their start and end apart: 9 -> 33, of which waited for: 6 -> 26; matrix products, arithmetic and copies ran while one was open for 0% -> 0% of each run, Pallas kernels for 23% -> 24%
where the time goes in v2:
time: 276 us; the launch traced here: 275 us
  starting transfers between devices  102 us (37%)
  Pallas kernels  96.5 us (35%)
  waiting for transfers between devices  60.7 us (22%)
  local copies, waits for them, and re-layouts  14.3 us (5%)
    pallas_call x2, Pallas kernels, inverse_factor(): call(cholesky_kernel, (1,), [pl.BlockSpec(memory_space=pltpu.SMEM)] + [wh...  46 us
    ppermute x8, starting transfers between devices, row_permute(): return lax.ppermute(x, 'row', pairs)  42.5 us
    ppermute x8, waiting for transfers between devices, row_permute(): return lax.ppermute(x, 'row', pairs)  30.4 us
    all_to_all x5, starting transfers between devices, exchange(): return lax.all_to_all(x, axis, 0, 0, tiled=True)  25 us
    ppermute x14, waiting for transfers between devices, chip_permute(): return lax.ppermute(x, 'col', pairs)  22.5 us
    ppermute x6, starting transfers between devices, core_permute(): return lax.ppermute(x, 'col', [(k, k ^ 1) for k in range(2 * SIDE)])  22.3 us
    unnamed x22, local copies, waits for them, and re-layouts  14.2 us
    ppermute x14, starting transfers between devices, chip_permute(): return lax.ppermute(x, 'col', pairs)  12.1 us
  transfers between devices with their start and end apart: 33, of which 26 were waited for; matrix products, arithmetic and copies ran while one was open for 0% of the time, Pallas kernels for 24%

profile of v2, /device:TPU:1, one launch (start us, length us, event | category | flops | bytes accessed | tf_op | source)
XLA Modules:
  0.0 274.9 jit_solution(9641226913849646812)
XLA Ops:
  0.7 1.6 copy-done.6
  2.2 4.8 %shard_map.50 = f32[512,256]{1,0:T(8,128)S(1)} custom-call(f32[512,2048]{1,0:T(8,128)} %m_ref.7, bf16[2,512,2048]{2,1,0:T(8,128)(2,1)} %g_ref.7, f32[2048,256]{1,0:T(8,128)S(1)} %copy-done.6), custom_call_target="tpu_custom_call" | custom-call | flops 1610612736 | bytes 8388608 | tf_op jit(solution)/shard_map/pallas_call | solution.py:76
  7.0 1.5 collective-permute-start
  11.1 1.8 collective-permute-start.3
  13.0 1.6 collective-permute-done.1
  14.6 2.2 collective-permute-done.3
  16.9 1.9 collective-permute-start.2
  18.8 1.9 collective-permute-done.4
  22.0 2.8 %collective-permute-start.5 = (f32[2,128,256]{2,1,0:T(8,128)S(1)}, f32[2,128,256]{2,1,0:T(8,128)S(1)}, u32[]{:S(2)}, u32[]{:S(2)}) collective-permute-start(f32[2,128,256]{2,1,0:T(8,128)S(1)} %pad_maximum_fusion.1), channel_id=1, source_target_pairs={{0,1},{1,0},{2,3},{3,2},{4,5},{5,4},{6,7},{7,6},{8,9},{9,8},{10,11... | collective-permute-start | bytes 786440 | tf_op jit(solution)/shard_map/ppermute | solution.py:464
  26.6 4.7 %shard_map.52 = f32[16,256,128]{2,1,0:T(8,128)S(1)} custom-call(bf16[2,256,512]{2,1,0:T(8,128)(2,1)S(1)} %get-tuple-element.24.pt_ref, f32[512,2048]{1,0:T(8,128)} %m_ref.7, bf16[2,512,2048]{2,1,0:T(8,128)(2,1)} %g_ref.7), custom_call_target="tpu_custom_call" | custom-call | flops 1610612736 | bytes 8388608 | tf_op jit(solution)/shard_map/pallas_call | solution.py:138
  32.6 7.8 %all-to-all-start = ((f32[16,256,128]{2,1,0:T(8,128)}), f32[16,256,128]{2,1,0:T(8,128)S(1)}, u32[]{:S(2)}, u32[]{:S(2)}) async-start(f32[16,256,128]{2,1,0:T(8,128)} %copy-done.3), calls=%async_computation | async-start | bytes 4194304 | tf_op jit(solution)/shard_map/all_to_all | solution.py:509
  40.4 1.4 collective-permute-start.6
  41.8 8.9 %collective-permute-done.6 = f32[32,256]{1,0:T(8,128)S(1)} collective-permute-done((f32[32,256]{1,0:T(8,128)S(1)}, f32[32,256]{1,0:T(8,128)S(1)}, u32[]{:S(2)}, u32[]{:S(2)}) %collective-permute-start.6) | collective-permute-done | bytes 32800 | tf_op jit(solution)/shard_map/ppermute | solution.py:455
  50.6 5.3 %collective-permute-start.7 = (f32[32,256]{1,0:T(8,128)S(1)}, f32[32,256]{1,0:T(8,128)S(1)}, u32[]{:S(2)}, u32[]{:S(2)}) collective-permute-start(f32[32,256]{1,0:T(8,128)S(1)} %add.86), channel_id=1, source_target_pairs={{0,24},{8,16},{16,8},{24,0},{32,56},{40,48},{48,40},{56,32},{64,88... | collective-permute-start | bytes 98312 | tf_op jit(solution)/shard_map/ppermute | solution.py:455
  55.9 2.7 collective-permute-done.7
  58.6 11.8 %collective-permute-start.8 = (f32[32,256]{1,0:T(8,128)S(1)}, f32[32,256]{1,0:T(8,128)S(1)}, u32[]{:S(2)}, u32[]{:S(2)}) collective-permute-start(f32[32,256]{1,0:T(8,128)S(1)} %add.87), channel_id=1, source_target_pairs={{0,32},{8,40},{16,48},{24,56},{32,0},{40,8},{48,16},{56,24},{64,96... | collective-permute-start | bytes 98312 | tf_op jit(solution)/shard_map/ppermute | solution.py:455
  71.7 3.0 %collective-permute-start.9 = (f32[32,256]{1,0:T(8,128)S(1)}, f32[32,256]{1,0:T(8,128)S(1)}, u32[]{:S(2)}, u32[]{:S(2)}) collective-permute-start(f32[32,256]{1,0:T(8,128)S(1)} %add.88), channel_id=1, source_target_pairs={{0,96},{8,104},{16,112},{24,120},{32,64},{40,72},{48,80},{56,88},{... | collective-permute-start | bytes 98312 | tf_op jit(solution)/shard_map/ppermute | solution.py:455
  76.0 5.3 %collective-permute-start.10 = (f32[32,256]{1,0:T(8,128)S(1)}, f32[32,256]{1,0:T(8,128)S(1)}, u32[]{:S(2)}, u32[]{:S(2)}) collective-permute-start(f32[32,256]{1,0:T(8,128)S(1)} %add.89), channel_id=1, source_target_pairs={{0,1},{1,0},{2,3},{3,2},{4,5},{5,4},{6,7},{7,6},{8,9},{9,8},{10,11... | collective-permute-start | bytes 98312 | tf_op jit(solution)/shard_map/ppermute | solution.py:464
  82.2 1.8 collective-permute-start.11
  87.1 1.7 collective-permute-done.12.refs_2_
  90.0 4.3 %all-to-all-start.1 = ((f32[16,256,128]{2,1,0:T(8,128)}), f32[16,256,128]{2,1,0:T(8,128)S(1)}, u32[]{:S(2)}, u32[]{:S(2)}) async-start(f32[16,256,128]{2,1,0:T(8,128)} %copy-done.1), calls=%async_computation.1 | async-start | bytes 4194304 | tf_op jit(solution)/shard_map/all_to_all | solution.py:509
  94.4 23.0 %shard_map.54.w_ref = f32[256,256]{1,0:T(8,128)S(1)} custom-call(s32[1]{0:T(128)} %bitcast.6.n_ref, f32[64,256]{1,0:T(8,128)S(1)} %maximum_select_fusion.2.refs_0_, f32[64,256]{1,0:T(8,128)S(1)} %collective-permute-done.11.refs_1_, f32[64,256]{1,0:T(8,128)S(1)} %collective-permute-done.12.refs_2_, f32[64,256]{1,0:T(8,128)S(1)} %collective-permute-done.13.refs_3_), custom_call_target="tpu_custom_call" | custom-call | flops 10000000000 | bytes 8388608 | tf_op jit(solution)/shard_map/pallas_call | solution.py:221
  117.4 2.5 all-to-all-done.1.x_ref
  119.9 8.0 %shard_map.55 = (f32[4,136,256]{2,1,0:T(8,128)S(1)}, f32[512,256]{1,0:T(8,128)S(1)}) custom-call(f32[512,256]{1,0:T(8,128)S(1)} %bitcast.34, f32[256,256]{1,0:T(8,128)S(1)} %shard_map.54.w_ref, f32[16,256,128]{2,1,0:T(8,128)S(1)} %all-to-all-done.1.x_ref, f32[512,2048]{1,0:T(8,128)} %m_ref.7, bf16[2,512,2048]{2,1,0:T(8,128)(2,1)} %g_ref.7), custom_call_target="tpu_custom_call" | custom-call | flops 2684354560 | bytes 8388608 | tf_op jit(solution)/shard_map/pallas_call | solution.py:274
  128.0 5.2 %collective-permute-start.14 = (f32[2,136,256]{2,1,0:T(8,128)S(1)}, f32[2,136,256]{2,1,0:T(8,128)S(1)}, u32[]{:S(2)}, u32[]{:S(2)}) collective-permute-start(f32[2,136,256]{2,1,0:T(8,128)S(1)} %constant_dynamic-slice_fusion), channel_id=1, source_target_pairs={{0,1},{1,0},{2,3},{3,2},{4,5},{5,4},{6,7},{7,6},{8,9},{9,8},{10,11... | collective-permute-start | bytes 835592 | tf_op jit(solution)/shard_map/ppermute | solution.py:464
  135.7 3.8 %collective-permute-done.15 = f32[136,256]{1,0:T(8,128)S(1)} collective-permute-done((f32[136,256]{1,0:T(8,128)S(1)}, f32[136,256]{1,0:T(8,128)S(1)}, u32[]{:S(2)}, u32[]{:S(2)}) %collective-permute-start.15) | collective-permute-done | bytes 139296 | tf_op jit(solution)/shard_map/ppermute | solution.py:460
  141.7 3.1 %collective-permute-done.18 = f32[136,256]{1,0:T(8,128)S(1)} collective-permute-done((f32[136,256]{1,0:T(8,128)S(1)}, f32[136,256]{1,0:T(8,128)S(1)}, u32[]{:S(2)}, u32[]{:S(2)}) %collective-permute-start.18) | collective-permute-done | bytes 139296 | tf_op jit(solution)/shard_map/ppermute | solution.py:460
  146.2 2.8 %collective-permute-start.19 = (f32[2,136,256]{2,1,0:T(8,128)S(1)}, f32[2,136,256]{2,1,0:T(8,128)S(1)}, u32[]{:S(2)}, u32[]{:S(2)}) collective-permute-start(f32[2,136,256]{2,1,0:T(8,128)S(1)} %pad_maximum_fusion), channel_id=1, source_target_pairs={{0,1},{1,0},{2,3},{3,2},{4,5},{5,4},{6,7},{7,6},{8,9},{9,8},{10,11... | collective-permute-start | bytes 835592 | tf_op jit(solution)/shard_map/ppermute | solution.py:464
  148.9 7.6 %shard_map.57 = (f32[256,2048]{1,0:T(8,128)S(1)}, f32[512,2048]{1,0:T(8,128)}) custom-call(f32[512,256]{1,0:T(8,128)S(1)} %get-tuple-element.33.o_ref, f32[256,256]{1,0:T(8,128)S(1)} %shard_map.54.w_ref, f32[16,256,128]{2,1,0:T(8,128)S(1)} %all-to-all-done.1.x_ref, f32[512,2048]{1,0:T(8,128)} %m_ref.7, bf16[2,512,2048]{2,1,0:T(8,128)(2,1)} %g_ref.7), custom_call_target="tpu_custom_call" | custom-call | flops 2415919104 | bytes 8388608 | tf_op jit(solution)/shard_map/pallas_call | solution.py:303
  158.5 4.3 %shard_map.58 = f32[16,256,128]{2,1,0:T(8,128)S(1)} custom-call(bf16[2,256,512]{2,1,0:T(8,128)(2,1)S(1)} %get-tuple-element.32.pt_ref, f32[512,2048]{1,0:T(8,128)} %get-tuple-element.34.b_ref), custom_call_target="tpu_custom_call" | custom-call | flops 1610612736 | bytes 8388608 | tf_op jit(solution)/shard_map/pallas_call | solution.py:138
  164.1 3.7 %all-to-all-start.2 = ((f32[16,256,128]{2,1,0:T(8,128)}), f32[16,256,128]{2,1,0:T(8,128)S(1)}, u32[]{:S(2)}, u32[]{:S(2)}) async-start(f32[16,256,128]{2,1,0:T(8,128)} %copy-done), calls=%async_computation.2 | async-start | bytes 4194304 | tf_op jit(solution)/shard_map/all_to_all | solution.py:509
  169.1 11.0 %collective-permute-done.20 = f32[32,256]{1,0:T(8,128)S(1)} collective-permute-done((f32[32,256]{1,0:T(8,128)S(1)}, f32[32,256]{1,0:T(8,128)S(1)}, u32[]{:S(2)}, u32[]{:S(2)}) %collective-permute-start.20) | collective-permute-done | bytes 32800 | tf_op jit(solution)/shard_map/ppermute | solution.py:455
  180.1 3.5 %collective-permute-start.21 = (f32[32,256]{1,0:T(8,128)S(1)}, f32[32,256]{1,0:T(8,128)S(1)}, u32[]{:S(2)}, u32[]{:S(2)}) collective-permute-start(f32[32,256]{1,0:T(8,128)S(1)} %add.97), channel_id=1, source_target_pairs={{0,24},{8,16},{16,8},{24,0},{32,56},{40,48},{48,40},{56,32},{64,88... | collective-permute-start | bytes 98312 | tf_op jit(solution)/shard_map/ppermute | solution.py:455
  183.6 2.6 collective-permute-done.21
  186.2 12.2 %collective-permute-start.22 = (f32[32,256]{1,0:T(8,128)S(1)}, f32[32,256]{1,0:T(8,128)S(1)}, u32[]{:S(2)}, u32[]{:S(2)}) collective-permute-start(f32[32,256]{1,0:T(8,128)S(1)} %add.98), channel_id=1, source_target_pairs={{0,32},{8,40},{16,48},{24,56},{32,0},{40,8},{48,16},{56,24},{64,96... | collective-permute-start | bytes 98312 | tf_op jit(solution)/shard_map/ppermute | solution.py:455
  199.7 4.2 %collective-permute-start.23 = (f32[32,256]{1,0:T(8,128)S(1)}, f32[32,256]{1,0:T(8,128)S(1)}, u32[]{:S(2)}, u32[]{:S(2)}) collective-permute-start(f32[32,256]{1,0:T(8,128)S(1)} %add.99), channel_id=1, source_target_pairs={{0,96},{8,104},{16,112},{24,120},{32,64},{40,72},{48,80},{56,88},{... | collective-permute-start | bytes 98312 | tf_op jit(solution)/shard_map/ppermute | solution.py:455
  205.2 4.7 %collective-permute-start.24 = (f32[32,256]{1,0:T(8,128)S(1)}, f32[32,256]{1,0:T(8,128)S(1)}, u32[]{:S(2)}, u32[]{:S(2)}) collective-permute-start(f32[32,256]{1,0:T(8,128)S(1)} %add.100), channel_id=1, source_target_pairs={{0,1},{1,0},{2,3},{3,2},{4,5},{5,4},{6,7},{7,6},{8,9},{9,8},{10,11... | collective-permute-start | bytes 98312 | tf_op jit(solution)/shard_map/ppermute | solution.py:464
  211.4 1.4 collective-permute-start.26
  216.0 1.8 collective-permute-done.27.refs_3_
  217.9 4.3 %all-to-all-start.3 = ((f32[16,256,128]{2,1,0:T(8,128)}), f32[16,256,128]{2,1,0:T(8,128)S(1)}, u32[]{:S(2)}, u32[]{:S(2)}) async-start(f32[16,256,128]{2,1,0:T(8,128)} %copy-done.2), calls=%async_computation.3 | async-start | bytes 4194304 | tf_op jit(solution)/shard_map/all_to_all | solution.py:509
  222.2 1.6 copy-done.8
  223.8 4.0 %shard_map.62.c_ref = f32[512,2048]{1,0:T(8,128)} custom-call(f32[512,256]{1,0:T(8,128)S(1)} %get-tuple-element.33.o_ref, f32[8,256]{1,0:T(8,128)S(1)} %get-tuple-element.44.rs_ref, f32[256,2048]{1,0:T(8,128)S(1)} %copy-done.8), custom_call_target="tpu_custom_call" | custom-call | flops 1610612736 | bytes 8388608 | tf_op jit(solution)/shard_map/pallas_call | solution.py:335
  227.8 23.0 %shard_map.60.w_ref = f32[256,256]{1,0:T(8,128)S(1)} custom-call(s32[1]{0:T(128)} %bitcast.6.n_ref, f32[64,256]{1,0:T(8,128)S(1)} %maximum_select_fusion.3.refs_0_, f32[64,256]{1,0:T(8,128)S(1)} %collective-permute-done.25.refs_1_, f32[64,256]{1,0:T(8,128)S(1)} %collective-permute-done.26.refs_2_, f32[64,256]{1,0:T(8,128)S(1)} %collective-permute-done.27.refs_3_), custom_call_target="tpu_custom_call" | custom-call | flops 10000000000 | bytes 8388608 | tf_op jit(solution)/shard_map/pallas_call | solution.py:221
  252.9 1.6 copy-done.5
  255.4 3.4 %shard_map.61 = (f32[256,2048]{1,0:T(8,128)S(1)}, f32[512,256]{1,0:T(8,128)S(1)}, f32[8,8,256]{2,1,0:T(8,128)}) custom-call(f32[512,256]{1,0:T(8,128)S(1)} %bitcast_multiply_fusion.p_ref, f32[256,256]{1,0:T(8,128)S(1)} %copy-done.10, f32[16,256,128]{2,1,0:T(8,128)S(1)} %copy-done.5), custom_call_target="tpu_custom_call" | custom-call | flops 805306368 | bytes 8388608 | tf_op jit(solution)/shard_map/pallas_call | solution.py:371
  258.8 4.9 %all-to-all-start.4 = ((f32[8,8,256]{2,1,0:T(8,128)}), f32[8,8,256]{2,1,0:T(8,128)S(1)}, u32[]{:S(2)}, u32[]{:S(2)}) async-start(f32[8,8,256]{2,1,0:T(8,128)} %get-tuple-element.41), calls=%async_computation.4 | async-start | bytes 131072 | tf_op jit(solution)/shard_map/all_to_all | solution.py:509
  263.7 5.8 %shard_map.64 = f32[512,2048]{1,0:T(8,128)} custom-call(f32[512,256]{1,0:T(8,128)S(1)} %get-tuple-element.40.o_ref, f32[256,2048]{1,0:T(8,128)S(1)} %get-tuple-element.42.raw_ref, f32[512,2048]{1,0:T(8,128)} %get-tuple-element.34.b_ref), custom_call_target="tpu_custom_call" | custom-call | flops 1610612736 | bytes 8388608 | tf_op jit(solution)/shard_map/pallas_call | solution.py:403
  269.5 5.4 %shard_map.63 = bf16[512,2048]{1,0:T(8,128)(2,1)} custom-call(f32[512,256]{1,0:T(8,128)S(1)} %get-tuple-element.40.o_ref, f32[8,8,256]{2,1,0:T(8,128)S(1)} %all-to-all-done.4.sq_ref, f32[256,2048]{1,0:T(8,128)S(1)} %get-tuple-element.42.raw_ref, f32[512,2048]{1,0:T(8,128)} %shard_map.62.c_ref), custom_call_target="tpu_custom_call" | custom-call | flops 1610612736 | bytes 8388608 | tf_op jit(solution)/shard_map/pallas_call | solution.py:430
  (85 shorter events, 35.8 us)
Async XLA Ops:
  0.6 1.6 copy-start.6
  7.0 2.7 collective-permute-start
  9.8 4.8 %collective-permute-start.1 = (f32[128,256]{1,0:T(8,128)S(1)}, f32[128,256]{1,0:T(8,128)S(1)}, u32[]{:S(2)}, u32[]{:S(2)}) collective-permute-start(f32[128,256]{1,0:T(8,128)S(1)} %get-tuple-element.52), channel_id=1, source_target_pairs={{0,2},{1,3},{2,0},{3,1},{4,6},{5,7},{6,4},{7,5},{8,10},{9,11},{10,... | collective-permute-start | bytes 393224 | tf_op jit(solution)/shard_map/ppermute | solution.py:460
  11.1 5.6 %collective-permute-start.3 = (f32[128,256]{1,0:T(8,128)S(1)}, f32[128,256]{1,0:T(8,128)S(1)}, u32[]{:S(2)}, u32[]{:S(2)}) collective-permute-start(f32[128,256]{1,0:T(8,128)S(1)} %get-tuple-element.53), channel_id=1, source_target_pairs={{0,6},{1,7},{2,4},{3,5},{4,2},{5,3},{6,0},{7,1},{8,14},{9,15},{10,... | collective-permute-start | bytes 393224 | tf_op jit(solution)/shard_map/ppermute | solution.py:460
  16.8 3.9 %collective-permute-start.4 = (f32[128,256]{1,0:T(8,128)S(1)}, f32[128,256]{1,0:T(8,128)S(1)}, u32[]{:S(2)}, u32[]{:S(2)}) collective-permute-start(f32[128,256]{1,0:T(8,128)S(1)} %get-tuple-element.51), channel_id=1, source_target_pairs={{0,2},{1,3},{2,0},{3,1},{4,6},{5,7},{6,4},{7,5},{8,10},{9,11},{10,... | collective-permute-start | bytes 393224 | tf_op jit(solution)/shard_map/ppermute | solution.py:460
  16.9 5.1 %collective-permute-start.2 = (f32[128,256]{1,0:T(8,128)S(1)}, f32[128,256]{1,0:T(8,128)S(1)}, u32[]{:S(2)}, u32[]{:S(2)}) collective-permute-start(f32[128,256]{1,0:T(8,128)S(1)} %get-tuple-element.50), channel_id=1, source_target_pairs={{0,6},{1,7},{2,4},{3,5},{4,2},{5,3},{6,0},{7,1},{8,14},{9,15},{10,... | collective-permute-start | bytes 393224 | tf_op jit(solution)/shard_map/ppermute | solution.py:460
  22.0 3.9 %collective-permute-start.5 = (f32[2,128,256]{2,1,0:T(8,128)S(1)}, f32[2,128,256]{2,1,0:T(8,128)S(1)}, u32[]{:S(2)}, u32[]{:S(2)}) collective-permute-start(f32[2,128,256]{2,1,0:T(8,128)S(1)} %pad_maximum_fusion.1), channel_id=1, source_target_pairs={{0,1},{1,0},{2,3},{3,2},{4,5},{5,4},{6,7},{7,6},{8,9},{9,8},{10,11... | collective-permute-start | bytes 786440 | tf_op jit(solution)/shard_map/ppermute | solution.py:464
  31.3 1.3 copy-start.3
  32.6 52.5 %all-to-all-start = ((f32[16,256,128]{2,1,0:T(8,128)}), f32[16,256,128]{2,1,0:T(8,128)S(1)}, u32[]{:S(2)}, u32[]{:S(2)}) async-start(f32[16,256,128]{2,1,0:T(8,128)} %copy-done.3), calls=%async_computation | async-start | bytes 4194304 | tf_op jit(solution)/shard_map/all_to_all | solution.py:509
  40.4 10.2 %collective-permute-start.6 = (f32[32,256]{1,0:T(8,128)S(1)}, f32[32,256]{1,0:T(8,128)S(1)}, u32[]{:S(2)}, u32[]{:S(2)}) collective-permute-start(f32[32,256]{1,0:T(8,128)S(1)} %get-tuple-element.23), channel_id=1, source_target_pairs={{0,8},{8,0},{16,24},{24,16},{32,40},{40,32},{48,56},{56,48},{64,72... | collective-permute-start | bytes 98312 | tf_op jit(solution)/shard_map/ppermute | solution.py:455
  50.6 8.0 %collective-permute-start.7 = (f32[32,256]{1,0:T(8,128)S(1)}, f32[32,256]{1,0:T(8,128)S(1)}, u32[]{:S(2)}, u32[]{:S(2)}) collective-permute-start(f32[32,256]{1,0:T(8,128)S(1)} %add.86), channel_id=1, source_target_pairs={{0,24},{8,16},{16,8},{24,0},{32,56},{40,48},{48,40},{56,32},{64,88... | collective-permute-start | bytes 98312 | tf_op jit(solution)/shard_map/ppermute | solution.py:455
  58.6 13.1 %collective-permute-start.8 = (f32[32,256]{1,0:T(8,128)S(1)}, f32[32,256]{1,0:T(8,128)S(1)}, u32[]{:S(2)}, u32[]{:S(2)}) collective-permute-start(f32[32,256]{1,0:T(8,128)S(1)} %add.87), channel_id=1, source_target_pairs={{0,32},{8,40},{16,48},{24,56},{32,0},{40,8},{48,16},{56,24},{64,96... | collective-permute-start | bytes 98312 | tf_op jit(solution)/shard_map/ppermute | solution.py:455
  71.7 4.3 %collective-permute-start.9 = (f32[32,256]{1,0:T(8,128)S(1)}, f32[32,256]{1,0:T(8,128)S(1)}, u32[]{:S(2)}, u32[]{:S(2)}) collective-permute-start(f32[32,256]{1,0:T(8,128)S(1)} %add.88), channel_id=1, source_target_pairs={{0,96},{8,104},{16,112},{24,120},{32,64},{40,72},{48,80},{56,88},{... | collective-permute-start | bytes 98312 | tf_op jit(solution)/shard_map/ppermute | solution.py:455
  76.0 6.2 %collective-permute-start.10 = (f32[32,256]{1,0:T(8,128)S(1)}, f32[32,256]{1,0:T(8,128)S(1)}, u32[]{:S(2)}, u32[]{:S(2)}) collective-permute-start(f32[32,256]{1,0:T(8,128)S(1)} %add.89), channel_id=1, source_target_pairs={{0,1},{1,0},{2,3},{3,2},{4,5},{5,4},{6,7},{7,6},{8,9},{9,8},{10,11... | collective-permute-start | bytes 98312 | tf_op jit(solution)/shard_map/ppermute | solution.py:464
  82.2 4.9 %collective-permute-start.11 = (f32[64,256]{1,0:T(8,128)S(1)}, f32[64,256]{1,0:T(8,128)S(1)}, u32[]{:S(2)}, u32[]{:S(2)}) collective-permute-start(f32[64,256]{1,0:T(8,128)S(1)} %maximum_select_fusion.2.refs_0_), channel_id=1, source_target_pairs={{0,6},{1,7},{2,0},{3,1},{4,2},{5,3},{6,4},{7,5},{8,14},{9,15},{10,... | collective-permute-start | bytes 196616 | tf_op jit(solution)/shard_map/ppermute | solution.py:460
  84.1 4.7 %collective-permute-start.12 = (f32[64,256]{1,0:T(8,128)S(1)}, f32[64,256]{1,0:T(8,128)S(1)}, u32[]{:S(2)}, u32[]{:S(2)}) collective-permute-start(f32[64,256]{1,0:T(8,128)S(1)} %maximum_select_fusion.2.refs_0_), channel_id=1, source_target_pairs={{0,4},{1,5},{2,6},{3,7},{4,0},{5,1},{6,2},{7,3},{8,12},{9,13},{10,... | collective-permute-start | bytes 196616 | tf_op jit(solution)/shard_map/ppermute | solution.py:460
  84.5 5.6 %collective-permute-start.13 = (f32[64,256]{1,0:T(8,128)S(1)}, f32[64,256]{1,0:T(8,128)S(1)}, u32[]{:S(2)}, u32[]{:S(2)}) collective-permute-start(f32[64,256]{1,0:T(8,128)S(1)} %maximum_select_fusion.2.refs_0_), channel_id=1, source_target_pairs={{0,2},{1,3},{2,4},{3,5},{4,6},{5,7},{6,0},{7,1},{8,10},{9,11},{10,... | collective-permute-start | bytes 196616 | tf_op jit(solution)/shard_map/ppermute | solution.py:460
  85.7 1.3 copy-start.1
  90.0 29.9 %all-to-all-start.1 = ((f32[16,256,128]{2,1,0:T(8,128)}), f32[16,256,128]{2,1,0:T(8,128)S(1)}, u32[]{:S(2)}, u32[]{:S(2)}) async-start(f32[16,256,128]{2,1,0:T(8,128)} %copy-done.1), calls=%async_computation.1 | async-start | bytes 4194304 | tf_op jit(solution)/shard_map/all_to_all | solution.py:509
  128.0 6.4 %collective-permute-start.14 = (f32[2,136,256]{2,1,0:T(8,128)S(1)}, f32[2,136,256]{2,1,0:T(8,128)S(1)}, u32[]{:S(2)}, u32[]{:S(2)}) collective-permute-start(f32[2,136,256]{2,1,0:T(8,128)S(1)} %constant_dynamic-slice_fusion), channel_id=1, source_target_pairs={{0,1},{1,0},{2,3},{3,2},{4,5},{5,4},{6,7},{7,6},{8,9},{9,8},{10,11... | collective-permute-start | bytes 835592 | tf_op jit(solution)/shard_map/ppermute | solution.py:464
  134.5 5.0 %collective-permute-start.15 = (f32[136,256]{1,0:T(8,128)S(1)}, f32[136,256]{1,0:T(8,128)S(1)}, u32[]{:S(2)}, u32[]{:S(2)}) collective-permute-start(f32[136,256]{1,0:T(8,128)S(1)} %get-tuple-element.48), channel_id=1, source_target_pairs={{0,2},{1,3},{2,0},{3,1},{4,6},{5,7},{6,4},{7,5},{8,10},{9,11},{10,... | collective-permute-start | bytes 417800 | tf_op jit(solution)/shard_map/ppermute | solution.py:460
  134.6 6.2 %collective-permute-start.17 = (f32[136,256]{1,0:T(8,128)S(1)}, f32[136,256]{1,0:T(8,128)S(1)}, u32[]{:S(2)}, u32[]{:S(2)}) collective-permute-start(f32[136,256]{1,0:T(8,128)S(1)} %get-tuple-element.49), channel_id=1, source_target_pairs={{0,6},{1,7},{2,4},{3,5},{4,2},{5,3},{6,0},{7,1},{8,14},{9,15},{10,... | collective-permute-start | bytes 417800 | tf_op jit(solution)/shard_map/ppermute | solution.py:460
  140.8 4.0 %collective-permute-start.18 = (f32[136,256]{1,0:T(8,128)S(1)}, f32[136,256]{1,0:T(8,128)S(1)}, u32[]{:S(2)}, u32[]{:S(2)}) collective-permute-start(f32[136,256]{1,0:T(8,128)S(1)} %get-tuple-element.47), channel_id=1, source_target_pairs={{0,2},{1,3},{2,0},{3,1},{4,6},{5,7},{6,4},{7,5},{8,10},{9,11},{10,... | collective-permute-start | bytes 417800 | tf_op jit(solution)/shard_map/ppermute | solution.py:460
  140.9 5.2 %collective-permute-start.16 = (f32[136,256]{1,0:T(8,128)S(1)}, f32[136,256]{1,0:T(8,128)S(1)}, u32[]{:S(2)}, u32[]{:S(2)}) collective-permute-start(f32[136,256]{1,0:T(8,128)S(1)} %get-tuple-element.46), channel_id=1, source_target_pairs={{0,6},{1,7},{2,4},{3,5},{4,2},{5,3},{6,0},{7,1},{8,14},{9,15},{10,... | collective-permute-start | bytes 417800 | tf_op jit(solution)/shard_map/ppermute | solution.py:460
  146.2 10.4 %collective-permute-start.19 = (f32[2,136,256]{2,1,0:T(8,128)S(1)}, f32[2,136,256]{2,1,0:T(8,128)S(1)}, u32[]{:S(2)}, u32[]{:S(2)}) collective-permute-start(f32[2,136,256]{2,1,0:T(8,128)S(1)} %pad_maximum_fusion), channel_id=1, source_target_pairs={{0,1},{1,0},{2,3},{3,2},{4,5},{5,4},{6,7},{7,6},{8,9},{9,8},{10,11... | collective-permute-start | bytes 835592 | tf_op jit(solution)/shard_map/ppermute | solution.py:464
  156.5 1.3 copy-start.7
  162.8 1.3 copy-start
  164.1 48.6 %all-to-all-start.2 = ((f32[16,256,128]{2,1,0:T(8,128)}), f32[16,256,128]{2,1,0:T(8,128)S(1)}, u32[]{:S(2)}, u32[]{:S(2)}) async-start(f32[16,256,128]{2,1,0:T(8,128)} %copy-done), calls=%async_computation.2 | async-start | bytes 4194304 | tf_op jit(solution)/shard_map/all_to_all | solution.py:509
  167.9 12.3 %collective-permute-start.20 = (f32[32,256]{1,0:T(8,128)S(1)}, f32[32,256]{1,0:T(8,128)S(1)}, u32[]{:S(2)}, u32[]{:S(2)}) collective-permute-start(f32[32,256]{1,0:T(8,128)S(1)} %get-tuple-element.31), channel_id=1, source_target_pairs={{0,8},{8,0},{16,24},{24,16},{32,40},{40,32},{48,56},{56,48},{64,72... | collective-permute-start | bytes 98312 | tf_op jit(solution)/shard_map/ppermute | solution.py:455
  180.1 6.1 %collective-permute-start.21 = (f32[32,256]{1,0:T(8,128)S(1)}, f32[32,256]{1,0:T(8,128)S(1)}, u32[]{:S(2)}, u32[]{:S(2)}) collective-permute-start(f32[32,256]{1,0:T(8,128)S(1)} %add.97), channel_id=1, source_target_pairs={{0,24},{8,16},{16,8},{24,0},{32,56},{40,48},{48,40},{56,32},{64,88... | collective-permute-start | bytes 98312 | tf_op jit(solution)/shard_map/ppermute | solution.py:455
  186.2 13.5 %collective-permute-start.22 = (f32[32,256]{1,0:T(8,128)S(1)}, f32[32,256]{1,0:T(8,128)S(1)}, u32[]{:S(2)}, u32[]{:S(2)}) collective-permute-start(f32[32,256]{1,0:T(8,128)S(1)} %add.98), channel_id=1, source_target_pairs={{0,32},{8,40},{16,48},{24,56},{32,0},{40,8},{48,16},{56,24},{64,96... | collective-permute-start | bytes 98312 | tf_op jit(solution)/shard_map/ppermute | solution.py:455
  199.7 5.5 %collective-permute-start.23 = (f32[32,256]{1,0:T(8,128)S(1)}, f32[32,256]{1,0:T(8,128)S(1)}, u32[]{:S(2)}, u32[]{:S(2)}) collective-permute-start(f32[32,256]{1,0:T(8,128)S(1)} %add.99), channel_id=1, source_target_pairs={{0,96},{8,104},{16,112},{24,120},{32,64},{40,72},{48,80},{56,88},{... | collective-permute-start | bytes 98312 | tf_op jit(solution)/shard_map/ppermute | solution.py:455
  205.2 5.5 %collective-permute-start.24 = (f32[32,256]{1,0:T(8,128)S(1)}, f32[32,256]{1,0:T(8,128)S(1)}, u32[]{:S(2)}, u32[]{:S(2)}) collective-permute-start(f32[32,256]{1,0:T(8,128)S(1)} %add.100), channel_id=1, source_target_pairs={{0,1},{1,0},{2,3},{3,2},{4,5},{5,4},{6,7},{7,6},{8,9},{9,8},{10,11... | collective-permute-start | bytes 98312 | tf_op jit(solution)/shard_map/ppermute | solution.py:464
  210.7 4.0 %collective-permute-start.25 = (f32[64,256]{1,0:T(8,128)S(1)}, f32[64,256]{1,0:T(8,128)S(1)}, u32[]{:S(2)}, u32[]{:S(2)}) collective-permute-start(f32[64,256]{1,0:T(8,128)S(1)} %maximum_select_fusion.3.refs_0_), channel_id=1, source_target_pairs={{0,6},{1,7},{2,0},{3,1},{4,2},{5,3},{6,4},{7,5},{8,14},{9,15},{10,... | collective-permute-start | bytes 196616 | tf_op jit(solution)/shard_map/ppermute | solution.py:460
  211.4 4.6 %collective-permute-start.26 = (f32[64,256]{1,0:T(8,128)S(1)}, f32[64,256]{1,0:T(8,128)S(1)}, u32[]{:S(2)}, u32[]{:S(2)}) collective-permute-start(f32[64,256]{1,0:T(8,128)S(1)} %maximum_select_fusion.3.refs_0_), channel_id=1, source_target_pairs={{0,4},{1,5},{2,6},{3,7},{4,0},{5,1},{6,2},{7,3},{8,12},{9,13},{10,... | collective-permute-start | bytes 196616 | tf_op jit(solution)/shard_map/ppermute | solution.py:460
  212.8 5.1 %collective-permute-start.27 = (f32[64,256]{1,0:T(8,128)S(1)}, f32[64,256]{1,0:T(8,128)S(1)}, u32[]{:S(2)}, u32[]{:S(2)}) collective-permute-start(f32[64,256]{1,0:T(8,128)S(1)} %maximum_select_fusion.3.refs_0_), channel_id=1, source_target_pairs={{0,2},{1,3},{2,4},{3,5},{4,6},{5,7},{6,0},{7,1},{8,10},{9,11},{10,... | collective-permute-start | bytes 196616 | tf_op jit(solution)/shard_map/ppermute | solution.py:460
  213.4 1.3 copy-start.2
  217.9 33.7 %all-to-all-start.3 = ((f32[16,256,128]{2,1,0:T(8,128)}), f32[16,256,128]{2,1,0:T(8,128)S(1)}, u32[]{:S(2)}, u32[]{:S(2)}) async-start(f32[16,256,128]{2,1,0:T(8,128)} %copy-done.2), calls=%async_computation.3 | async-start | bytes 4194304 | tf_op jit(solution)/shard_map/all_to_all | solution.py:509
  222.2 1.6 copy-start.8
  250.8 0.7 copy-start.9
  251.5 1.3 copy-start.4
  252.9 1.6 copy-start.5
  254.4 0.9 copy-start.10
  258.8 10.7 %all-to-all-start.4 = ((f32[8,8,256]{2,1,0:T(8,128)}), f32[8,8,256]{2,1,0:T(8,128)S(1)}, u32[]{:S(2)}, u32[]{:S(2)}) async-start(f32[8,8,256]{2,1,0:T(8,128)} %get-tuple-element.41), calls=%async_computation.4 | async-start | bytes 131072 | tf_op jit(solution)/shard_map/all_to_all | solution.py:509

commit v3 on v2

--- a/solution.py
+++ b/solution.py
@@ -52,6 +52,10 @@
     )
 
 
+def in_hbm(*arrays):
+    return [pltpu.with_memory_space_constraint(a, pltpu.HBM) for a in arrays]
+
+
 def whole(shape):
     return pl.BlockSpec(shape, lambda i: (0,) * len(shape))
 
@@ -85,52 +89,57 @@
         jax.ShapeDtypeStruct((rows, rank), F32),
         [],
         6 * rows * cols * rank,
-    )(momentum, grads, basis)
-
-
-def gram_kernel(n_ref, p_ref, pt_ref, c_ref, scratch):
+    )(*in_hbm(momentum, grads, basis))
+
+
+def gram_kernel(n_ref, p_ref, pt_ref, c_ref, t):
     turned = p_ref[...].T
-    scratch[...] = turned
     pt_ref[0], pt_ref[1] = split(turned)
+    p, half = p_ref[...], LANES
+    t[: 2 * half] = exact(turned, p[:, :half], NN)
+    t[2 * half :] = exact(turned[half:], p[:, half:], NN)
     size = c_ref.shape[0]
-    first = pl.multiple_of(n_ref[0] * size, size)
-    c_ref[...] = exact(scratch[pl.ds(first, size), :], p_ref[...], NN)
+    c_ref[...] = t[pl.ds(pl.multiple_of(n_ref[0] * size, size), size), :]
 
 
 def gram_part(p, index, parts):
     rows, rank = p.shape
+    height = 3 * LANES
     return call(
         gram_kernel,
         (1,),
         [pl.BlockSpec(memory_space=pltpu.SMEM), whole(p.shape)],
-        [whole((2, rank, rows)), whole((rank // parts, rank))],
+        [whole((2, rank, rows)), whole((height // parts, LANES))],
         [
             jax.ShapeDtypeStruct((2, rank, rows), BF16),
-            jax.ShapeDtypeStruct((rank // parts, rank), F32),
-        ],
-        [pltpu.VMEM((rank, rows), F32)],
+            jax.ShapeDtypeStruct((height // parts, LANES), F32),
+        ],
+        [pltpu.VMEM((height, LANES), F32)],
         2 * rows * rank * rank,
     )(index, p)
 
 
-def store_products(pt_ref, b, x_ref):
+def store_products(pt_ref, c_ref, b, x_ref):
+    rank = pt_ref.shape[1]
     r = dot3((pt_ref[0], pt_ref[1]), split(b), NN)
     for k in range(x_ref.shape[0]):
-        x_ref[k] = r[:, k * LANES : (k + 1) * LANES]
-
-
-def raw_first_kernel(pt_ref, m_ref, g_ref, x_ref):
-    store_products(pt_ref, m_ref[...] + g_ref[0].astype(F32), x_ref)
-
-
-def raw_second_kernel(pt_ref, b_ref, x_ref):
-    store_products(pt_ref, b_ref[...], x_ref)
-
-
-def raw_products(kernel, pt, bigs):
+        x_ref[k, :rank] = r[:, k * LANES : (k + 1) * LANES]
+        x_ref[k, rank:] = c_ref[...]
+
+
+def raw_first_kernel(pt_ref, c_ref, m_ref, g_ref, x_ref):
+    store_products(pt_ref, c_ref, m_ref[...] + g_ref[0].astype(F32), x_ref)
+
+
+def raw_second_kernel(pt_ref, c_ref, b_ref, x_ref):
+    store_products(pt_ref, c_ref, b_ref[...], x_ref)
+
+
+def raw_products(kernel, pt, part, bigs):
     _, rank, rows = pt.shape
     cols = bigs[0].shape[1]
     bn = cols // GRID
+    height = rank + part.shape[0]
     specs = [
         pl.BlockSpec((rows, bn), lambda i: (0, i)),
         pl.BlockSpec((1, rows, bn), lambda i: (0, 0, i)),
@@ -138,15 +147,16 @@
     return call(
         kernel,
         (GRID,),
-        [whole(pt.shape)] + specs[: len(bigs)],
-        pl.BlockSpec((bn // LANES, rank, LANES), lambda i: (i, 0, 0)),
-        jax.ShapeDtypeStruct((cols // LANES, rank, LANES), F32),
+        [whole(pt.shape), whole(part.shape)] + specs[: len(bigs)],
+        pl.BlockSpec((bn // LANES, height, LANES), lambda i: (i, 0, 0)),
+        pltpu.HBM((cols // LANES, height, LANES), F32),
         [],
         6 * rows * cols * rank,
-    )(pt, *bigs)
-
-
-def spread_kernel(x_ref, y_ref):
+    )(pt, part, *in_hbm(*bigs))
+
+
+def spread_kernel(x_ref, *refs):
+    tails, (y_ref, t_ref) = refs[:-2], refs[-2:]
     count = x_ref.shape[0]
     total = x_ref[0]
     for k in range(1, count):
@@ -154,13 +164,37 @@
     for k in range(count):
         y_ref[k] = total
 
-
-def spread_sum(x):
+    @pl.when(pl.program_id(0) == 0)
+    def _():
+        for n, tail in enumerate(tails):
+            size = tail.shape[1]
+            total = tail[0]
+            for k in range(1, count):
+                total = total + tail[k]
+            t_ref[n * size : (n + 1) * size] = total
+
+
+def spread_sum(x, rank):
     count, height, width = x.shape
-    spec = pl.BlockSpec((count, height // 4, width), lambda i: (0, i, 0))
-    return call(
-        spread_kernel, (4,), [spec], spec, jax.ShapeDtypeStruct(x.shape, F32), [], count * height * width
-    )(x)
+    size = 16
+    steps = 4
+    tails = [
+        pl.BlockSpec((count, size, width), lambda i, n=n: (0, rank // size + n, 0))
+        for n in range((height - rank) // size)
+    ]
+    spec = pl.BlockSpec((count, rank // steps, width), lambda i: (0, i, 0))
+    return call(
+        spread_kernel,
+        (steps,),
+        [spec] + tails,
+        [spec, whole((height - rank, width))],
+        [
+            pltpu.HBM((count, rank, width), F32),
+            jax.ShapeDtypeStruct((height - rank, width), F32),
+        ],
+        [],
+        count * height * width,
+    )(*[x] * (1 + len(tails)))
 
 
 def eliminated(m):
@@ -168,17 +202,27 @@
     lane = lax.broadcasted_iota(jnp.int32, (8, n), 1)
     sub = lax.broadcasted_iota(jnp.int32, (8, n), 0)
     tiles = [m[8 * t : 8 * t + 8] for t in range(n // 8)]
-    for j in range(n):
+    for j in range(0, n, 2):
         t, r = divmod(j, 8)
-        row = tiles[t][r : r + 1]
-        inv = 1.0 / row[:, j : j + 1]
-        here = lane == j
-        scaled = jnp.where(here[:1], inv, row * inv)
+        first, second = lane[:1] == j, lane[:1] == j + 1
+        both = (lane >= j) & (lane < j + 2)
+        row0, row1 = tiles[t][r : r + 1], tiles[t][r + 1 : r + 2]
+        a, b = row0[:, j : j + 1], row0[:, j + 1 : j + 2]
+        inv_a = 1.0 / a
+        ratio = b * inv_a
+        d = row1[:, j + 1 : j + 2] - b * ratio
+        inv_d = 1.0 / d
+        low = row1 - ratio * row0
+        unit = jnp.where(first, -ratio, jnp.where(second, 1.0, low))
+        use1 = unit * inv_d
+        use0 = jnp.where(first, 1.0, jnp.where(second, 0.0, row0)) * inv_a - ratio * use1
+        kept = jnp.where(first, -ratio, jnp.where(second, d, low))
         for s in range(t, n // 8):
-            column = jnp.broadcast_to(tiles[s][:, j : j + 1], (8, n))
-            new = jnp.where(here, 0.0, tiles[s]) - column * scaled
+            c0 = jnp.broadcast_to(tiles[s][:, j : j + 1], (8, n))
+            c1 = jnp.broadcast_to(tiles[s][:, j + 1 : j + 2], (8, n))
+            new = jnp.where(both, 0.0, tiles[s]) - c0 * use0 - c1 * use1
             if s == t:
-                new = jnp.where(sub > r, new, tiles[s])
+                new = jnp.where(sub > r + 1, new, jnp.where(sub == r + 1, kept, tiles[s]))
             tiles[s] = new
     m = jnp.concatenate(tiles, axis=0)
     i = lax.broadcasted_iota(jnp.int32, (n, n), 0)
@@ -198,14 +242,14 @@
     half = LANES
 
     def body(b, carry):
+        w = eliminated(a[pl.ds(pl.multiple_of(2 * b * half, half), half), :])
         first = pl.multiple_of(b * half, half)
-        w = eliminated(a[pl.ds(first, half), pl.ds(first, half)])
         w_ref[pl.ds(first, half), pl.ds(first, half)] = w
 
         @pl.when(b == 0)
         def _():
-            low[...] = exact(a[half:, :half], w, NT)
-            a[half:, half:] -= exact(low[...], low[...], NT)
+            low[...] = exact(a[half : 2 * half], w, NT)
+            a[2 * half :] -= exact(low[...], low[...], NT)
 
         return carry
 
@@ -217,14 +261,14 @@
 
 
 def inverse_factor(pieces, index):
-    rank = pieces[0].shape[1]
+    rank = 2 * LANES
     return call(
         cholesky_kernel,
         (1,),
         [pl.BlockSpec(memory_space=pltpu.SMEM)] + [whole(q.shape) for q in pieces],
         whole((rank, rank)),
         jax.ShapeDtypeStruct((rank, rank), F32),
-        [pltpu.VMEM((rank, rank), F32), pltpu.VMEM((LANES, LANES), F32)],
+        [pltpu.VMEM((3 * LANES, LANES), F32), pltpu.VMEM((LANES, LANES), F32)],
         10**10,
     )(index, *pieces)
 
@@ -285,7 +329,7 @@
         [jax.ShapeDtypeStruct(shape, F32), jax.ShapeDtypeStruct((rows, rank), F32)],
         [pltpu.VMEM((rows, rank), F32), pltpu.VMEM((rank, rank), F32)],
         10 * rows * cols * rank,
-    )(p, w, x, momentum, grads)
+    )(p, w, x, *in_hbm(momentum, grads))
 
 
 def update_kernel(o_ref, w_ref, x_ref, m_ref, g_ref, raw_ref, b_ref):
@@ -314,13 +358,10 @@
             pl.BlockSpec((rank, bn), lambda i: (0, i)),
             pl.BlockSpec((rows, bn), lambda i: (0, i)),
         ],
-        [
-            jax.ShapeDtypeStruct((rank, cols), F32),
-            jax.ShapeDtypeStruct((rows, cols), F32),
-        ],
+        [pltpu.HBM((rank, cols), F32), pltpu.HBM((rows, cols), F32)],
         [],
         9 * rows * cols * rank,
-    )(o, w, x, momentum, grads)
+    )(o, w, x, *in_hbm(momentum, grads))
 
 
 def change_kernel(factor, o_ref, rs_ref, raw_ref, c_ref):
@@ -337,10 +378,10 @@
         (GRID,),
         [whole(o.shape), whole(rs.shape), pl.BlockSpec((rank, bn), lambda i: (0, i))],
         pl.BlockSpec((rows, bn), lambda i: (0, i)),
-        jax.ShapeDtypeStruct((rows, cols), F32),
+        pltpu.HBM((rows, cols), F32),
         [],
         6 * rows * cols * rank,
-    )(o, rs, raw)
+    )(o, rs, *in_hbm(raw))
 
 
 def last_raw_kernel(p_ref, w_ref, x_ref, raw_ref, o_ref, sq_ref, total):
@@ -388,7 +429,7 @@
         ],
         [pltpu.VMEM((rank, LANES), F32)],
         3 * rows * cols * rank,
-    )(p, w, x)
+    )(p, w, *in_hbm(x))
 
 
 def state_kernel(o_ref, raw_ref, b_ref, s_ref):
@@ -412,7 +453,7 @@
         jax.ShapeDtypeStruct((rows, cols), F32),
         [],
         6 * rows * cols * rank,
-    )(o, raw, b)
+    )(o, raw, *in_hbm(b))
 
 
 def last_change_kernel(factor, o_ref, sq_ref, raw_ref, c_ref, out_ref):
@@ -440,19 +481,10 @@
         jax.ShapeDtypeStruct((rows, cols), BF16),
         [],
         6 * rows * cols * rank,
-    )(o, sq, raw, change)
+    )(o, sq, raw, *in_hbm(change))
 
 
 SIDE = 4
-
-
-def row_permute(x, move):
-    pairs = []
-    for y in range(SIDE):
-        for z in range(SIDE):
-            to = move(y, z)
-            pairs.append((SIDE * y + z, SIDE * to[0] + to[1]))
-    return lax.ppermute(x, "row", pairs)
 
 
 def chip_permute(x, move):
@@ -487,14 +519,7 @@
     )
 
 
-def gram_sum(part):
-    for move in (
-        lambda y, z: (y, near(z)),
-        lambda y, z: (y, far(z)),
-        lambda y, z: (near(y), z),
-        lambda y, z: (far(y), z),
-    ):
-        part = part + row_permute(part, move)
+def by_chip(part):
     core = lax.axis_index("col") % 2
     other = core_permute(part)
     chip = jnp.where(
@@ -509,12 +534,11 @@
     return lax.all_to_all(x, axis, 0, 0, tiled=True)
 
 
-def row_total(products, part, chip):
-    pieces = gram_sum(part)
-    own = spread_sum(exchange(products, "row"))
-    pieces, own = lax.optimization_barrier((pieces, own))
+def row_total(products, rank, chip, beside):
+    got, beside = lax.optimization_barrier((exchange(products, "row"), beside))
+    own, part = spread_sum(got, rank)
     total = exchange(own, "row")
-    return total, inverse_factor(pieces, chip)
+    return total, inverse_factor(by_chip(part), chip), beside
 
 
 def shards(momentum, grads, basis):
@@ -528,17 +552,17 @@
     p1 = first_projection(momentum, grads, basis)
     p1 = col_sum(p1.reshape(4, rows // 4, rank)).reshape(rows, rank)
     pt1, part1 = gram_part(p1, place, peers)
-    x1 = raw_products(raw_first_kernel, pt1, [momentum, grads])
-    x1, w1 = row_total(x1, part1, chip)
+    x1 = raw_products(raw_first_kernel, pt1, part1, [momentum, grads])
+    x1, w1, _ = row_total(x1, rank, chip, [])
     q2, o1 = middle(p1, w1, x1, momentum, grads)
     raw1, b2 = second_buffer(o1, w1, x1, momentum, grads)
     q2 = col_sum(q2)
     rs1 = lax.rsqrt(q2[0, rows // 4 :] + NORM_EPS)
     p2 = q2[:, : rows // 4].reshape(rows, rank) * rs1[:1]
     pt2, part2 = gram_part(p2, place, peers)
-    x2 = raw_products(raw_second_kernel, pt2, [b2])
+    x2 = raw_products(raw_second_kernel, pt2, part2, [b2])
     change1 = first_change(factor, o1, rs1, raw1)
-    x2, w2 = row_total(x2, part2, chip)
+    x2, w2, change1 = row_total(x2, rank, chip, change1)
     raw2, o2, sq2 = last_raw(p2, w2, x2, peers)
     sq2 = exchange(sq2, "col")
     state = last_state(o2, raw2, b2)

time: 276 us -> 254 us (0.920)
  starting transfers between devices: 102 us -> 48.3 us
  blocking collectives: 0 us -> 38.7 us
  local copies, waits for them, and re-layouts: 14.3 us -> 0.13 us
  Pallas kernels: 96.5 us -> 107 us
  waiting for transfers between devices: 60.7 us -> 57.5 us
    ppermute x8 -> x0, starting transfers between devices: 42.5 us -> none  [row_permute(): return lax.ppermute(x, 'row', pairs)]
    all_to_all x0 -> x1, blocking collectives: none -> 38.7 us  [exchange(): return lax.all_to_all(x, axis, 0, 0, tiled=True)]
    ppermute x8 -> x0, waiting for transfers between devices: 30.4 us -> none  [row_permute(): return lax.ppermute(x, 'row', pairs)]
    all_to_all x5 -> x4, waiting for transfers between devices: 2.52 us -> 28.1 us  [exchange(): return lax.all_to_all(x, axis, 0, 0, tiled=True)]
    unnamed x22 -> x0, local copies, waits for them, and re-layouts: 14.2 us -> none
    ppermute x6, starting transfers between devices: 22.3 us -> 11.9 us  [core_permute(): return lax.ppermute(x, 'col', [(k, k ^ 1) for k in range(2 * SIDE)])]
    pallas_call x4, Pallas kernels: 10.3 us -> 15.5 us  [the longest x2 11.3 us: raw_products(): call(kernel, (GRID,), [whole(pt.shape), whole(part.shape)] + specs[:len(b...]
    all_to_all x5 -> x4, starting transfers between devices: 25 us -> 23.4 us  [exchange(): return lax.all_to_all(x, axis, 0, 0, tiled=True)]
  transfers between devices with their start and end apart: 33 -> 24, of which waited for: 26 -> 20; matrix products, arithmetic and copies ran while one was open for 0% -> 0% of each run, Pallas kernels for 24% -> 26%
where the time goes in v3:
time: 254 us; the launch traced here: 253 us
  Pallas kernels  107 us (42%)
  waiting for transfers between devices  57.5 us (23%)
  starting transfers between devices  48.3 us (19%)
  blocking collectives  38.7 us (15%)
    pallas_call x2, Pallas kernels, inverse_factor(): call(cholesky_kernel, (1,), [pl.BlockSpec(memory_space=pltpu.SMEM)] + [wh...  46.7 us
    all_to_all x1, blocking collectives, exchange(): return lax.all_to_all(x, axis, 0, 0, tiled=True)  38.7 us
    all_to_all x4, waiting for transfers between devices, exchange(): return lax.all_to_all(x, axis, 0, 0, tiled=True)  28.1 us
    ppermute x14, waiting for transfers between devices, chip_permute(): return lax.ppermute(x, 'col', pairs)  24.3 us
    all_to_all x4, starting transfers between devices, exchange(): return lax.all_to_all(x, axis, 0, 0, tiled=True)  23.4 us
    ppermute x14, starting transfers between devices, chip_permute(): return lax.ppermute(x, 'col', pairs)  12.9 us
    ppermute x6, starting transfers between devices, core_permute(): return lax.ppermute(x, 'col', [(k, k ^ 1) for k in range(2 * SIDE)])  11.9 us
    pallas_call x2, Pallas kernels, raw_products(): call(kernel, (GRID,), [whole(pt.shape), whole(part.shape)] + specs[:len(b...  11.3 us
  transfers between devices with their start and end apart: 24, of which 20 were waited for; matrix products, arithmetic and copies ran while one was open for 0% of the time, Pallas kernels for 26%

profile of v3, /device:TPU:1, one launch (start us, length us, event | category | flops | bytes accessed | tf_op | source)
XLA Modules:
  0.0 252.7 jit_solution(1215520128825373120)
XLA Ops:
  0.6 5.2 %shard_map.50 = f32[512,256]{1,0:T(8,128)S(1)} custom-call(f32[512,2048]{1,0:T(8,128)} %m_ref.7, bf16[2,512,2048]{2,1,0:T(8,128)(2,1)} %g_ref.7, f32[2048,256]{1,0:T(8,128)} %v_ref.1), custom_call_target="tpu_custom_call" | custom-call | flops 1610612736 | bytes 8388608 | tf_op jit(solution)/shard_map/pallas_call | solution.py:80
  5.9 1.5 collective-permute-start
  7.4 1.2 collective-permute-done
  8.6 1.4 collective-permute-start.1
  10.0 1.8 collective-permute-start.3
  11.8 1.6 collective-permute-done.1
  13.4 2.2 collective-permute-done.3
  15.7 1.9 collective-permute-start.2
  17.6 1.9 collective-permute-done.4
  19.5 1.3 collective-permute-done.2
  20.9 2.8 %collective-permute-start.5 = (f32[2,128,256]{2,1,0:T(8,128)S(1)}, f32[2,128,256]{2,1,0:T(8,128)S(1)}, u32[]{:S(2)}, u32[]{:S(2)}) collective-permute-start(f32[2,128,256]{2,1,0:T(8,128)S(1)} %pad_maximum_fusion.1), channel_id=1, source_target_pairs={{0,1},{1,0},{2,3},{3,2},{4,5},{5,4},{6,7},{7,6},{8,9},{9,8},{10,11... | collective-permute-start | bytes 786440 | tf_op jit(solution)/shard_map/ppermute | solution.py:496
  23.6 1.2 collective-permute-done.5
  25.7 5.9 %shard_map.52 = f32[16,304,128]{2,1,0:T(8,128)} custom-call(bf16[2,256,512]{2,1,0:T(8,128)(2,1)S(1)} %get-tuple-element.19.pt_ref, f32[48,128]{1,0:T(8,128)S(1)} %get-tuple-element.20.c_ref, f32[512,2048]{1,0:T(8,128)} %m_ref.7, bf16[2,512,2048]{2,1,0:T(8,128)(2,1)} %g_ref.7), custom_call_target="tpu_custom_call" | custom-call | flops 1610612736 | bytes 8388608 | tf_op jit(solution)/shard_map/pallas_call | solution.py:147
  31.5 38.7 %all_to_all.25.x_ref.refs_0_.refs_1_.refs_2_ = f32[16,304,128]{2,1,0:T(8,128)S(1)} all-to-all(f32[16,304,128]{2,1,0:T(8,128)} %shard_map.52), channel_id=1, replica_groups=mesh['row'=16,'col'=8] {'row'}, dimensions={0} | all-to-all | bytes 4980736 | tf_op jit(solution)/shard_map/all_to_all | solution.py:534
  70.2 2.1 shard_map.53
  72.3 4.2 %all-to-all-start.1 = ((f32[16,256,128]{2,1,0:T(8,128)}), f32[16,256,128]{2,1,0:T(8,128)S(1)}, u32[]{:S(2)}, u32[]{:S(2)}) async-start(f32[16,256,128]{2,1,0:T(8,128)} %get-tuple-element.22), calls=%async_computation.1 | async-start | bytes 4194304 | tf_op jit(solution)/shard_map/all_to_all | solution.py:534
  76.5 1.9 collective-permute-start.6
  78.4 0.8 collective-permute-done.6
  79.3 1.8 collective-permute-start.7
  82.5 3.3 %collective-permute-done.8.refs_2_ = f32[96,128]{1,0:T(8,128)S(1)} collective-permute-done((f32[96,128]{1,0:T(8,128)S(1)}, f32[96,128]{1,0:T(8,128)S(1)}, u32[]{:S(2)}, u32[]{:S(2)}) %collective-permute-start.8) | collective-permute-done | bytes 49184 | tf_op jit(solution)/shard_map/ppermute | solution.py:492
  86.4 23.3 %shard_map.54.w_ref = f32[256,256]{1,0:T(8,128)S(1)} custom-call(s32[1]{0:T(128)} %bitcast.6.n_ref, f32[96,128]{1,0:T(8,128)S(1)} %maximum_select_fusion.2.refs_0_, f32[96,128]{1,0:T(8,128)S(1)} %collective-permute-done.7.refs_1_, f32[96,128]{1,0:T(8,128)S(1)} %collective-permute-done.8.refs_2_, f32[96,128]{1,0:T(8,128)S(1)} %collective-permute-done.9.refs_3_), custom_call_target="tpu_custom_call" | custom-call | flops 10000000000 | bytes 8388608 | tf_op jit(solution)/shard_map/pallas_call | solution.py:265
  109.7 8.0 %shard_map.55 = (f32[4,136,256]{2,1,0:T(8,128)S(1)}, f32[512,256]{1,0:T(8,128)S(1)}) custom-call(f32[512,256]{1,0:T(8,128)S(1)} %bitcast.34, f32[256,256]{1,0:T(8,128)S(1)} %shard_map.54.w_ref, f32[16,256,128]{2,1,0:T(8,128)S(1)} %all-to-all-done.1.x_ref, f32[512,2048]{1,0:T(8,128)} %m_ref.7, bf16[2,512,2048]{2,1,0:T(8,128)(2,1)} %g_ref.7), custom_call_target="tpu_custom_call" | custom-call | flops 2684354560 | bytes 8388608 | tf_op jit(solution)/shard_map/pallas_call | solution.py:318
  117.8 1.6 collective-permute-start.10
  119.4 1.2 collective-permute-done.10
  120.7 1.5 collective-permute-start.13
  122.2 3.4 %collective-permute-done.11 = f32[136,256]{1,0:T(8,128)S(1)} collective-permute-done((f32[136,256]{1,0:T(8,128)S(1)}, f32[136,256]{1,0:T(8,128)S(1)}, u32[]{:S(2)}, u32[]{:S(2)}) %collective-permute-start.11) | collective-permute-done | bytes 139296 | tf_op jit(solution)/shard_map/ppermute | solution.py:492
  125.6 1.3 collective-permute-done.13
  127.0 1.2 collective-permute-start.12
  128.2 2.7 %collective-permute-done.14 = f32[136,256]{1,0:T(8,128)S(1)} collective-permute-done((f32[136,256]{1,0:T(8,128)S(1)}, f32[136,256]{1,0:T(8,128)S(1)}, u32[]{:S(2)}, u32[]{:S(2)}) %collective-permute-start.14) | collective-permute-done | bytes 139296 | tf_op jit(solution)/shard_map/ppermute | solution.py:492
  130.9 1.3 collective-permute-done.12
  132.3 2.8 %collective-permute-start.15 = (f32[2,136,256]{2,1,0:T(8,128)S(1)}, f32[2,136,256]{2,1,0:T(8,128)S(1)}, u32[]{:S(2)}, u32[]{:S(2)}) collective-permute-start(f32[2,136,256]{2,1,0:T(8,128)S(1)} %pad_maximum_fusion), channel_id=1, source_target_pairs={{0,1},{1,0},{2,3},{3,2},{4,5},{5,4},{6,7},{7,6},{8,9},{9,8},{10,11... | collective-permute-start | bytes 835592 | tf_op jit(solution)/shard_map/ppermute | solution.py:496
  135.1 7.9 %shard_map.57 = (f32[256,2048]{1,0:T(8,128)}, f32[512,2048]{1,0:T(8,128)}) custom-call(f32[512,256]{1,0:T(8,128)S(1)} %get-tuple-element.26.o_ref, f32[256,256]{1,0:T(8,128)S(1)} %shard_map.54.w_ref, f32[16,256,128]{2,1,0:T(8,128)S(1)} %all-to-all-done.1.x_ref, f32[512,2048]{1,0:T(8,128)} %m_ref.7, bf16[2,512,2048]{2,1,0:T(8,128)(2,1)} %g_ref.7), custom_call_target="tpu_custom_call" | custom-call | flops 2415919104 | bytes 8388608 | tf_op jit(solution)/shard_map/pallas_call | solution.py:347
  144.0 5.4 %shard_map.58 = f32[16,304,128]{2,1,0:T(8,128)} custom-call(bf16[2,256,512]{2,1,0:T(8,128)(2,1)S(1)} %get-tuple-element.24.pt_ref, f32[48,128]{1,0:T(8,128)S(1)} %get-tuple-element.25.c_ref, f32[512,2048]{1,0:T(8,128)} %get-tuple-element.27.b_ref), custom_call_target="tpu_custom_call" | custom-call | flops 1610612736 | bytes 8388608 | tf_op jit(solution)/shard_map/pallas_call | solution.py:147
  149.5 6.9 %all-to-all-start.2 = ((f32[16,304,128]{2,1,0:T(8,128)}), f32[16,304,128]{2,1,0:T(8,128)S(1)}, u32[]{:S(2)}, u32[]{:S(2)}) async-start(f32[16,304,128]{2,1,0:T(8,128)} %shard_map.58), calls=%async_computation.2 | async-start | bytes 4980736 | tf_op jit(solution)/shard_map/all_to_all | solution.py:534
  156.3 5.5 %shard_map.59.c_ref = f32[512,2048]{1,0:T(8,128)} custom-call(f32[512,256]{1,0:T(8,128)S(1)} %get-tuple-element.26.o_ref, f32[8,256]{1,0:T(8,128)S(1)} %get-tuple-element.36.rs_ref, f32[256,2048]{1,0:T(8,128)} %get-tuple-element.28.raw_ref), custom_call_target="tpu_custom_call" | custom-call | flops 1610612736 | bytes 8388608 | tf_op jit(solution)/shard_map/pallas_call | solution.py:376
  161.8 28.1 %all-to-all-done.2.x_ref.refs_0_.refs_1_.refs_2_ = f32[16,304,128]{2,1,0:T(8,128)S(1)} async-done(((f32[16,304,128]{2,1,0:T(8,128)}), f32[16,304,128]{2,1,0:T(8,128)S(1)}, u32[]{:S(2)}, u32[]{:S(2)}) %all-to-all-start.2) | async-done | bytes 2490400 | tf_op jit(solution)/shard_map/all_to_all | solution.py:534
  189.9 2.1 shard_map.60
  192.0 7.3 %all-to-all-start.3 = ((f32[16,256,128]{2,1,0:T(8,128)}), f32[16,256,128]{2,1,0:T(8,128)}, u32[]{:S(2)}, u32[]{:S(2)}) async-start(f32[16,256,128]{2,1,0:T(8,128)} %get-tuple-element.31), calls=%async_computation.3 | async-start | bytes 4194304 | tf_op jit(solution)/shard_map/all_to_all | solution.py:534
  199.3 1.5 collective-permute-start.16
  200.8 0.8 collective-permute-done.16
  201.6 1.1 collective-permute-start.17
  203.7 1.3 collective-permute-done.17.refs_1_
  205.0 2.6 %collective-permute-done.18.refs_2_ = f32[96,128]{1,0:T(8,128)S(1)} collective-permute-done((f32[96,128]{1,0:T(8,128)S(1)}, f32[96,128]{1,0:T(8,128)S(1)}, u32[]{:S(2)}, u32[]{:S(2)}) %collective-permute-start.18) | collective-permute-done | bytes 49184 | tf_op jit(solution)/shard_map/ppermute | solution.py:492
  208.1 23.3 %shard_map.61.w_ref = f32[256,256]{1,0:T(8,128)S(1)} custom-call(s32[1]{0:T(128)} %bitcast.6.n_ref, f32[96,128]{1,0:T(8,128)S(1)} %maximum_select_fusion.3.refs_0_, f32[96,128]{1,0:T(8,128)S(1)} %collective-permute-done.17.refs_1_, f32[96,128]{1,0:T(8,128)S(1)} %collective-permute-done.18.refs_2_, f32[96,128]{1,0:T(8,128)S(1)} %collective-permute-done.19.refs_3_), custom_call_target="tpu_custom_call" | custom-call | flops 10000000000 | bytes 8388608 | tf_op jit(solution)/shard_map/pallas_call | solution.py:265
  231.4 5.0 %shard_map.62 = (f32[256,2048]{1,0:T(8,128)S(1)}, f32[512,256]{1,0:T(8,128)S(1)}, f32[8,8,256]{2,1,0:T(8,128)}) custom-call(f32[512,256]{1,0:T(8,128)S(1)} %bitcast_multiply_fusion.p_ref, f32[256,256]{1,0:T(8,128)S(1)} %shard_map.61.w_ref, f32[16,256,128]{2,1,0:T(8,128)} %all-to-all-done.3.x_ref), custom_call_target="tpu_custom_call" | custom-call | flops 805306368 | bytes 8388608 | tf_op jit(solution)/shard_map/pallas_call | solution.py:412
  236.4 5.0 %all-to-all-start.4 = ((f32[8,8,256]{2,1,0:T(8,128)}), f32[8,8,256]{2,1,0:T(8,128)S(1)}, u32[]{:S(2)}, u32[]{:S(2)}) async-start(f32[8,8,256]{2,1,0:T(8,128)} %get-tuple-element.33), calls=%async_computation.4 | async-start | bytes 131072 | tf_op jit(solution)/shard_map/all_to_all | solution.py:534
  241.4 5.8 %shard_map.64 = f32[512,2048]{1,0:T(8,128)} custom-call(f32[512,256]{1,0:T(8,128)S(1)} %get-tuple-element.32.o_ref, f32[256,2048]{1,0:T(8,128)S(1)} %get-tuple-element.34.raw_ref, f32[512,2048]{1,0:T(8,128)} %get-tuple-element.27.b_ref), custom_call_target="tpu_custom_call" | custom-call | flops 1610612736 | bytes 8388608 | tf_op jit(solution)/shard_map/pallas_call | solution.py:444
  247.2 5.4 %shard_map.63 = bf16[512,2048]{1,0:T(8,128)(2,1)} custom-call(f32[512,256]{1,0:T(8,128)S(1)} %get-tuple-element.32.o_ref, f32[8,8,256]{2,1,0:T(8,128)S(1)} %all-to-all-done.4.sq_ref, f32[256,2048]{1,0:T(8,128)S(1)} %get-tuple-element.34.raw_ref, f32[512,2048]{1,0:T(8,128)} %shard_map.59.c_ref), custom_call_target="tpu_custom_call" | custom-call | flops 1610612736 | bytes 8388608 | tf_op jit(solution)/shard_map/pallas_call | solution.py:471
  (38 shorter events, 6.0 us)
Async XLA Ops:
  5.9 2.7 %collective-permute-start = (f32[2,128,256]{2,1,0:T(8,128)S(1)}, f32[2,128,256]{2,1,0:T(8,128)S(1)}, u32[]{:S(2)}, u32[]{:S(2)}) collective-permute-start(f32[2,128,256]{2,1,0:T(8,128)S(1)} %constant_dynamic-slice_fusion.1), channel_id=1, source_target_pairs={{0,1},{1,0},{2,3},{3,2},{4,5},{5,4},{6,7},{7,6},{8,9},{9,8},{10,11... | collective-permute-start | bytes 786440 | tf_op jit(solution)/shard_map/ppermute | solution.py:496
  8.6 4.8 %collective-permute-start.1 = (f32[128,256]{1,0:T(8,128)S(1)}, f32[128,256]{1,0:T(8,128)S(1)}, u32[]{:S(2)}, u32[]{:S(2)}) collective-permute-start(f32[128,256]{1,0:T(8,128)S(1)} %get-tuple-element.44), channel_id=1, source_target_pairs={{0,2},{1,3},{2,0},{3,1},{4,6},{5,7},{6,4},{7,5},{8,10},{9,11},{10,... | collective-permute-start | bytes 393224 | tf_op jit(solution)/shard_map/ppermute | solution.py:492
  10.0 5.6 %collective-permute-start.3 = (f32[128,256]{1,0:T(8,128)S(1)}, f32[128,256]{1,0:T(8,128)S(1)}, u32[]{:S(2)}, u32[]{:S(2)}) collective-permute-start(f32[128,256]{1,0:T(8,128)S(1)} %get-tuple-element.45), channel_id=1, source_target_pairs={{0,6},{1,7},{2,4},{3,5},{4,2},{5,3},{6,0},{7,1},{8,14},{9,15},{10,... | collective-permute-start | bytes 393224 | tf_op jit(solution)/shard_map/ppermute | solution.py:492
  15.6 3.9 %collective-permute-start.4 = (f32[128,256]{1,0:T(8,128)S(1)}, f32[128,256]{1,0:T(8,128)S(1)}, u32[]{:S(2)}, u32[]{:S(2)}) collective-permute-start(f32[128,256]{1,0:T(8,128)S(1)} %get-tuple-element.43), channel_id=1, source_target_pairs={{0,2},{1,3},{2,0},{3,1},{4,6},{5,7},{6,4},{7,5},{8,10},{9,11},{10,... | collective-permute-start | bytes 393224 | tf_op jit(solution)/shard_map/ppermute | solution.py:492
  15.7 5.1 %collective-permute-start.2 = (f32[128,256]{1,0:T(8,128)S(1)}, f32[128,256]{1,0:T(8,128)S(1)}, u32[]{:S(2)}, u32[]{:S(2)}) collective-permute-start(f32[128,256]{1,0:T(8,128)S(1)} %get-tuple-element.42), channel_id=1, source_target_pairs={{0,6},{1,7},{2,4},{3,5},{4,2},{5,3},{6,0},{7,1},{8,14},{9,15},{10,... | collective-permute-start | bytes 393224 | tf_op jit(solution)/shard_map/ppermute | solution.py:492
  20.9 3.9 %collective-permute-start.5 = (f32[2,128,256]{2,1,0:T(8,128)S(1)}, f32[2,128,256]{2,1,0:T(8,128)S(1)}, u32[]{:S(2)}, u32[]{:S(2)}) collective-permute-start(f32[2,128,256]{2,1,0:T(8,128)S(1)} %pad_maximum_fusion.1), channel_id=1, source_target_pairs={{0,1},{1,0},{2,3},{3,2},{4,5},{5,4},{6,7},{7,6},{8,9},{9,8},{10,11... | collective-permute-start | bytes 786440 | tf_op jit(solution)/shard_map/ppermute | solution.py:496
  72.3 37.4 %all-to-all-start.1 = ((f32[16,256,128]{2,1,0:T(8,128)}), f32[16,256,128]{2,1,0:T(8,128)S(1)}, u32[]{:S(2)}, u32[]{:S(2)}) async-start(f32[16,256,128]{2,1,0:T(8,128)} %get-tuple-element.22), calls=%async_computation.1 | async-start | bytes 4194304 | tf_op jit(solution)/shard_map/all_to_all | solution.py:534
  76.5 2.7 %collective-permute-start.6 = (f32[48,128]{1,0:T(8,128)S(1)}, f32[48,128]{1,0:T(8,128)S(1)}, u32[]{:S(2)}, u32[]{:S(2)}) collective-permute-start(f32[48,128]{1,0:T(8,128)S(1)} %get-tuple-element.21), channel_id=1, source_target_pairs={{0,1},{1,0},{2,3},{3,2},{4,5},{5,4},{6,7},{7,6},{8,9},{9,8},{10,11... | collective-permute-start | bytes 73736 | tf_op jit(solution)/shard_map/ppermute | solution.py:496
  79.3 3.2 %collective-permute-start.7 = (f32[96,128]{1,0:T(8,128)S(1)}, f32[96,128]{1,0:T(8,128)S(1)}, u32[]{:S(2)}, u32[]{:S(2)}) collective-permute-start(f32[96,128]{1,0:T(8,128)S(1)} %maximum_select_fusion.2.refs_0_), channel_id=1, source_target_pairs={{0,6},{1,7},{2,0},{3,1},{4,2},{5,3},{6,4},{7,5},{8,14},{9,15},{10,... | collective-permute-start | bytes 147464 | tf_op jit(solution)/shard_map/ppermute | solution.py:492
  81.1 4.7 %collective-permute-start.8 = (f32[96,128]{1,0:T(8,128)S(1)}, f32[96,128]{1,0:T(8,128)S(1)}, u32[]{:S(2)}, u32[]{:S(2)}) collective-permute-start(f32[96,128]{1,0:T(8,128)S(1)} %maximum_select_fusion.2.refs_0_), channel_id=1, source_target_pairs={{0,4},{1,5},{2,6},{3,7},{4,0},{5,1},{6,2},{7,3},{8,12},{9,13},{10,... | collective-permute-start | bytes 147464 | tf_op jit(solution)/shard_map/ppermute | solution.py:492
  81.5 4.8 %collective-permute-start.9 = (f32[96,128]{1,0:T(8,128)S(1)}, f32[96,128]{1,0:T(8,128)S(1)}, u32[]{:S(2)}, u32[]{:S(2)}) collective-permute-start(f32[96,128]{1,0:T(8,128)S(1)} %maximum_select_fusion.2.refs_0_), channel_id=1, source_target_pairs={{0,2},{1,3},{2,4},{3,5},{4,6},{5,7},{6,0},{7,1},{8,10},{9,11},{10,... | collective-permute-start | bytes 147464 | tf_op jit(solution)/shard_map/ppermute | solution.py:492
  117.8 2.7 %collective-permute-start.10 = (f32[2,136,256]{2,1,0:T(8,128)S(1)}, f32[2,136,256]{2,1,0:T(8,128)S(1)}, u32[]{:S(2)}, u32[]{:S(2)}) collective-permute-start(f32[2,136,256]{2,1,0:T(8,128)S(1)} %constant_dynamic-slice_fusion), channel_id=1, source_target_pairs={{0,1},{1,0},{2,3},{3,2},{4,5},{5,4},{6,7},{7,6},{8,9},{9,8},{10,11... | collective-permute-start | bytes 835592 | tf_op jit(solution)/shard_map/ppermute | solution.py:496
  120.6 5.0 %collective-permute-start.11 = (f32[136,256]{1,0:T(8,128)S(1)}, f32[136,256]{1,0:T(8,128)S(1)}, u32[]{:S(2)}, u32[]{:S(2)}) collective-permute-start(f32[136,256]{1,0:T(8,128)S(1)} %get-tuple-element.40), channel_id=1, source_target_pairs={{0,2},{1,3},{2,0},{3,1},{4,6},{5,7},{6,4},{7,5},{8,10},{9,11},{10,... | collective-permute-start | bytes 417800 | tf_op jit(solution)/shard_map/ppermute | solution.py:492
  120.7 6.2 %collective-permute-start.13 = (f32[136,256]{1,0:T(8,128)S(1)}, f32[136,256]{1,0:T(8,128)S(1)}, u32[]{:S(2)}, u32[]{:S(2)}) collective-permute-start(f32[136,256]{1,0:T(8,128)S(1)} %get-tuple-element.41), channel_id=1, source_target_pairs={{0,6},{1,7},{2,4},{3,5},{4,2},{5,3},{6,0},{7,1},{8,14},{9,15},{10,... | collective-permute-start | bytes 417800 | tf_op jit(solution)/shard_map/ppermute | solution.py:492
  126.9 4.0 %collective-permute-start.14 = (f32[136,256]{1,0:T(8,128)S(1)}, f32[136,256]{1,0:T(8,128)S(1)}, u32[]{:S(2)}, u32[]{:S(2)}) collective-permute-start(f32[136,256]{1,0:T(8,128)S(1)} %get-tuple-element.39), channel_id=1, source_target_pairs={{0,2},{1,3},{2,0},{3,1},{4,6},{5,7},{6,4},{7,5},{8,10},{9,11},{10,... | collective-permute-start | bytes 417800 | tf_op jit(solution)/shard_map/ppermute | solution.py:492
  127.0 5.2 %collective-permute-start.12 = (f32[136,256]{1,0:T(8,128)S(1)}, f32[136,256]{1,0:T(8,128)S(1)}, u32[]{:S(2)}, u32[]{:S(2)}) collective-permute-start(f32[136,256]{1,0:T(8,128)S(1)} %get-tuple-element.38), channel_id=1, source_target_pairs={{0,6},{1,7},{2,4},{3,5},{4,2},{5,3},{6,0},{7,1},{8,14},{9,15},{10,... | collective-permute-start | bytes 417800 | tf_op jit(solution)/shard_map/ppermute | solution.py:492
  132.3 10.7 %collective-permute-start.15 = (f32[2,136,256]{2,1,0:T(8,128)S(1)}, f32[2,136,256]{2,1,0:T(8,128)S(1)}, u32[]{:S(2)}, u32[]{:S(2)}) collective-permute-start(f32[2,136,256]{2,1,0:T(8,128)S(1)} %pad_maximum_fusion), channel_id=1, source_target_pairs={{0,1},{1,0},{2,3},{3,2},{4,5},{5,4},{6,7},{7,6},{8,9},{9,8},{10,11... | collective-permute-start | bytes 835592 | tf_op jit(solution)/shard_map/ppermute | solution.py:496
  149.5 40.4 %all-to-all-start.2 = ((f32[16,304,128]{2,1,0:T(8,128)}), f32[16,304,128]{2,1,0:T(8,128)S(1)}, u32[]{:S(2)}, u32[]{:S(2)}) async-start(f32[16,304,128]{2,1,0:T(8,128)} %shard_map.58), calls=%async_computation.2 | async-start | bytes 4980736 | tf_op jit(solution)/shard_map/all_to_all | solution.py:534
  192.0 39.4 %all-to-all-start.3 = ((f32[16,256,128]{2,1,0:T(8,128)}), f32[16,256,128]{2,1,0:T(8,128)}, u32[]{:S(2)}, u32[]{:S(2)}) async-start(f32[16,256,128]{2,1,0:T(8,128)} %get-tuple-element.31), calls=%async_computation.3 | async-start | bytes 4194304 | tf_op jit(solution)/shard_map/all_to_all | solution.py:534
  199.3 2.3 collective-permute-start.16
  201.6 3.3 %collective-permute-start.17 = (f32[96,128]{1,0:T(8,128)S(1)}, f32[96,128]{1,0:T(8,128)S(1)}, u32[]{:S(2)}, u32[]{:S(2)}) collective-permute-start(f32[96,128]{1,0:T(8,128)S(1)} %maximum_select_fusion.3.refs_0_), channel_id=1, source_target_pairs={{0,6},{1,7},{2,0},{3,1},{4,2},{5,3},{6,4},{7,5},{8,14},{9,15},{10,... | collective-permute-start | bytes 147464 | tf_op jit(solution)/shard_map/ppermute | solution.py:492
  202.7 4.8 %collective-permute-start.18 = (f32[96,128]{1,0:T(8,128)S(1)}, f32[96,128]{1,0:T(8,128)S(1)}, u32[]{:S(2)}, u32[]{:S(2)}) collective-permute-start(f32[96,128]{1,0:T(8,128)S(1)} %maximum_select_fusion.3.refs_0_), channel_id=1, source_target_pairs={{0,4},{1,5},{2,6},{3,7},{4,0},{5,1},{6,2},{7,3},{8,12},{9,13},{10,... | collective-permute-start | bytes 147464 | tf_op jit(solution)/shard_map/ppermute | solution.py:492
  203.4 4.6 %collective-permute-start.19 = (f32[96,128]{1,0:T(8,128)S(1)}, f32[96,128]{1,0:T(8,128)S(1)}, u32[]{:S(2)}, u32[]{:S(2)}) collective-permute-start(f32[96,128]{1,0:T(8,128)S(1)} %maximum_select_fusion.3.refs_0_), channel_id=1, source_target_pairs={{0,2},{1,3},{2,4},{3,5},{4,6},{5,7},{6,0},{7,1},{8,10},{9,11},{10,... | collective-permute-start | bytes 147464 | tf_op jit(solution)/shard_map/ppermute | solution.py:492
  236.4 10.8 %all-to-all-start.4 = ((f32[8,8,256]{2,1,0:T(8,128)}), f32[8,8,256]{2,1,0:T(8,128)S(1)}, u32[]{:S(2)}, u32[]{:S(2)}) async-start(f32[8,8,256]{2,1,0:T(8,128)} %get-tuple-element.33), calls=%async_computation.4 | async-start | bytes 131072 | tf_op jit(solution)/shard_map/all_to_all | solution.py:534
